TPU v7x, 512 devices: a whole 4x4x16 slice. The times are simulated.
512 devices in a mesh: tok: 64 (over z_hi, y, x), head: 8 (over z_lo, core).
Axes of the slice: x: 4, y: 4, z: 16 (z_hi: 4, z_lo: 4; z = z_hi * 4 + z_lo), core: 2. Of those that a mesh axis runs over, the one named last changes fastest.
Arguments:
- hidden_in: bfloat16 [16384, 2560], P('tok'), may hold values from -6 to 6
- norm_gain: float32 [2560], replicated, may hold values from 0.1 to 1.9
- w_qkv: bfloat16 [2560, 3840], P('tok', 'head'), may hold values from -4 to 4
- w_out: bfloat16 [2560, 2560], P('head', 'tok'), may hold values from -0.625 to 0.625
- prefill_cache: bfloat16 [8, 4096, 8, 1280], P(None, 'tok', 'head'), may hold values from -6 to 6
- lengths: int32 [8], replicated, may hold values from 1 to 4096, 20480 in all
- prefill_table: int32 [4096], replicated, may hold values from 0 to 4095, as said below
- decode_table: int32 [4096], replicated, may hold values from 0 to 4095, as said below
Outputs:
- attn_out: bfloat16 [16384, 2560], P('tok', 'head')
- decode_cache: bfloat16 [8, 4096, 8, 1280], P(None, 'tok', 'head')
Inputs may be any that keep to these rules, and one draw needn't show every extreme that they name: `prefill_table`: each prefill slot holds exactly one logical block. `decode_table`: the block in prefill slot s * 64 + k goes to decode slot d * 64 + k, where d - s modulo the size of tok depends only on k and each residue occurs for exactly 1 values of k.
All inputs are finite; a program needn't handle non-finite values.
Results may differ from a plain program's by a relative error of at most 0.015.
The roundings to bfloat16 on the way count: a program that leaves them out, or rounds other values in their place, can miss the bound.
Values may be sent and summed in bfloat16 or wider, within the bound.
A program may use at most 64 MiB of HBM per device.

v0:
```python
import math

import jax
import jax.numpy as jnp
from jax import lax
from jax.sharding import PartitionSpec as P

HD = 80
QPK = 4
BLK = 8


NORM_EPS = 1e-05
ROPE_BASE = 1000000.0


def rotary(vectors, positions):
    half_width = vectors.shape[-1] // 2
    frequency = ROPE_BASE ** (-2.0 * jnp.arange(half_width, dtype=jnp.float32) / vectors.shape[-1])
    angles = positions.astype(jnp.float32)[:, None] * frequency[None, :]
    cosine = jnp.cos(angles)[:, None, :]
    sines = jnp.sin(angles)[:, None, :]
    front_half = vectors[..., :half_width]
    back_half = vectors[..., half_width:]
    return jnp.concatenate(
        [front_half * cosine - back_half * sines, back_half * cosine + front_half * sines], axis=-1
    )


def attend(hidden_in, norm_gain, w_qkv):
    tok_rows = hidden_in.shape[0]
    my_index = lax.axis_index("tok")
    float_rows = hidden_in.astype(jnp.float32)
    normed = (
        float_rows
        * lax.rsqrt(jnp.mean(float_rows * float_rows, axis=-1, keepdims=True) + NORM_EPS)
        * norm_gain
    ).astype(jnp.bfloat16)
    projected = jnp.dot(
        normed, lax.all_gather(w_qkv, "tok", axis=0, tiled=True), preferred_element_type=jnp.float32
    )
    kv_local = w_qkv.shape[1] // ((QPK + 2) * HD)
    projected = projected.reshape(tok_rows, kv_local, QPK + 2, HD)
    row_index = jnp.arange(tok_rows, dtype=jnp.int32)
    positions = my_index * tok_rows + row_index
    queries = (
        rotary(projected[:, :, :QPK].reshape(tok_rows, kv_local * QPK, HD), positions)
        .astype(jnp.bfloat16)
        .reshape(tok_rows, kv_local * QPK * HD)
    )
    key_rows = (
        rotary(projected[:, :, QPK], positions)
        .astype(jnp.bfloat16)
        .reshape(tok_rows, kv_local * HD)
    )
    values = projected[:, :, QPK + 1].astype(jnp.bfloat16).reshape(tok_rows, kv_local * HD)
    query_grid = (
        queries.reshape(tok_rows, kv_local, QPK, HD)
        .transpose(1, 2, 0, 3)
        .reshape(kv_local, QPK * tok_rows, HD)
    )
    query_pos = jnp.tile(positions, QPK)
    last_row = jnp.max(positions)
    scale_factor = 1.0 / math.sqrt(HD)

    def key_positions(block_start, count):
        whole_rows = block_start + jnp.arange(count, dtype=jnp.int32)
        return whole_rows

    initial = (
        jnp.full((kv_local, QPK * tok_rows), -1e30, jnp.float32),
        jnp.zeros((kv_local, QPK * tok_rows), jnp.float32),
        jnp.zeros((kv_local, QPK * tok_rows, HD), jnp.float32),
    )
    key_part = lax.all_gather(key_rows, "tok", axis=0, tiled=True)
    value_part = lax.all_gather(values, "tok", axis=0, tiled=True)
    row_count = key_part.shape[0]
    step_rows = math.gcd(row_count, 512)
    key_grid = key_part.reshape(row_count, kv_local, HD)
    value_grid = value_part.reshape(row_count, kv_local, HD)

    def advance(step_index, status):
        offset = step_index * step_rows
        key_pos = key_positions(offset, step_rows)

        def update(current):
            running, denominator, weighted = current
            key_block = lax.dynamic_slice_in_dim(key_grid, offset, step_rows, 0)
            value_block = lax.dynamic_slice_in_dim(value_grid, offset, step_rows, 0)
            scores = (
                jnp.einsum(
                    "hqd,khd->hqk", query_grid, key_block, preferred_element_type=jnp.float32
                )
                * scale_factor
            )
            allowed = (key_pos[None, :] <= query_pos[:, None])[None]
            masked = jnp.where(allowed, scores, -1e30)
            highest = jnp.maximum(running, jnp.max(masked, axis=-1))
            expo_terms = jnp.where(allowed, jnp.exp(masked - highest[..., None]), 0.0)
            shrink = jnp.exp(running - highest)
            denominator = denominator * shrink + jnp.sum(expo_terms, axis=-1)
            weighted = weighted * shrink[..., None] + jnp.einsum(
                "hqk,khd->hqd",
                expo_terms.astype(jnp.bfloat16),
                value_block,
                preferred_element_type=jnp.float32,
            )
            return (highest, denominator, weighted)

        return lax.cond(jnp.min(key_pos) > last_row, lambda unchanged: unchanged, update, status)

    running, denominator, weighted = lax.fori_loop(0, row_count // step_rows, advance, initial)
    context = (
        (weighted / denominator[..., None])
        .reshape(kv_local, QPK, tok_rows, HD)
        .transpose(2, 0, 1, 3)
    )
    context = context.reshape(tok_rows, kv_local * QPK * HD).astype(jnp.bfloat16)
    return context


def project_out(context, w_out):
    partial_value = jnp.dot(
        context,
        lax.all_gather(w_out, "tok", axis=1, tiled=True),
        preferred_element_type=jnp.float32,
    )
    return lax.psum_scatter(
        partial_value.astype(jnp.bfloat16), "head", scatter_dimension=1, tiled=True
    )


def hand_over(prefill_cache, lengths, prefill_table, decode_table):
    tok_count = lax.axis_size("tok")
    my_index = lax.axis_index("tok")
    layers, slot_count, kv_local, extent = prefill_cache.shape
    block_total = prefill_table.shape[0]
    request_count = lengths.shape[0]
    per_request = block_total // request_count
    every_block = jnp.arange(block_total, dtype=jnp.int32)
    logical_of = jnp.zeros((block_total,), jnp.int32).at[prefill_table].set(every_block)
    held_here = lax.dynamic_slice_in_dim(logical_of, my_index * slot_count, slot_count)
    request = held_here // per_request
    request_len = jnp.sum(
        jnp.where(
            request[:, None] == jnp.arange(request_count, dtype=jnp.int32)[None, :],
            lengths[None, :],
            0,
        ),
        axis=1,
    )
    live_rows = (held_here % per_request * BLK)[:, None] + jnp.arange(BLK, dtype=jnp.int32)[
        None, :
    ] < request_len[:, None]
    masked = prefill_cache.reshape(layers, slot_count, kv_local, BLK, extent // BLK) * live_rows[
        None, :, None, :, None
    ].astype(jnp.bfloat16)
    masked = masked.reshape(layers, slot_count, kv_local, extent)
    target = decode_table[held_here] // slot_count
    send_order = jnp.argsort(target * slot_count + jnp.arange(slot_count, dtype=jnp.int32))
    outgoing = jnp.take(masked, send_order, axis=1)
    per_peer = slot_count // tok_count
    decode_of = jnp.zeros((block_total,), jnp.int32).at[decode_table].set(every_block)
    arriving = lax.dynamic_slice_in_dim(decode_of, my_index * slot_count, slot_count)
    anchor = prefill_table[arriving]
    position = jnp.argsort(jnp.argsort(anchor))
    collected = []
    for layer_index in range(layers):
        sending = outgoing[layer_index].reshape(tok_count, per_peer, kv_local, extent)
        received = lax.all_to_all(sending, "tok", split_axis=0, concat_axis=0, tiled=True)
        collected.append(received.reshape(slot_count, kv_local, extent))
    incoming = jnp.stack(collected)
    return jnp.take(incoming, position, axis=1)


def on_device(
    hidden_in, norm_gain, w_qkv, w_out, prefill_cache, lengths, prefill_table, decode_table
):
    context = attend(hidden_in, norm_gain, w_qkv)
    attn_out = project_out(context, w_out)
    decode_cache = hand_over(prefill_cache, lengths, prefill_table, decode_table)
    return (attn_out, decode_cache)


def solution(mesh):
    in_specs = (
        P("tok", None),
        P(),
        P("tok", "head"),
        P("head", "tok"),
        P(None, "tok", "head", None),
        P(),
        P(),
        P(),
    )
    out_specs = (P("tok", "head"), P(None, "tok", "head", None))
    return jax.shard_map(
        on_device, mesh=mesh, in_specs=in_specs, out_specs=out_specs, check_vma=False
    )
```

profile of v0, /device:TPU:64, one launch (start us, length us, event | category | flops | bytes accessed | tf_op | source)
XLA Modules:
  0.0 723.5 jit_solution(4846801455397867306)
XLA Ops:
  8.0 1.7 fusion.24
  9.7 124.3 %all-gather.6.cloned.1.call-done = bf16[2560,480]{1,0:T(8,128)(2,1)} async-done(((bf16[40,480]{1,0:T(8,128)(2,1)}), bf16[2560,480]{1,0:T(8,128)(2,1)}) %all-gather.6.cloned.1.call-update) | async-done | bytes 2457616 | tf_op jit(solution)/shard_map/all_gather | solution.py:40
  134.0 3.4 fusion.27
  139.1 15.5 %scatter_custom_fusion = s32[4096]{0:T(1024)S(1)} fusion(s32[4096]{0:T(1024)S(1)} %compare_select_fusion.3, s32[4096]{0:T(1024)S(1)} %iota.52, s32[]{:T(128)} %copy.199), kind=kCustom, calls=%fused_computation.84 | custom fusion | bytes 16388 | tf_op jit(solution)/shard_map/scatter | solution.py:141
  154.6 15.5 %scatter_custom_fusion.1 = s32[4096]{0:T(1024)S(1)} fusion(s32[4096]{0:T(1024)S(1)} %compare_select_fusion.2, s32[4096]{0:T(1024)S(1)} %iota.55, s32[]{:T(128)} %copy.199), kind=kCustom, calls=%fused_computation.82 | custom fusion | bytes 16388 | tf_op jit(solution)/shard_map/scatter | solution.py:163
  171.7 2.0 sort.45
  175.5 2.4 slice_bitcast_fusion
  180.8 10.3 %all-to-all-start = ((bf16[64,2,640]{2,1,0:T(2,128)(2,1)}), bf16[64,2,640]{2,1,0:T(2,128)(2,1)S(1)}, u32[]{:S(2)}, u32[]{:S(2)}) async-start(bf16[64,2,640]{2,1,0:T(2,128)(2,1)} %reshape.360), calls=%async_computation.1 | async-start | bytes 327680 | tf_op jit(solution)/shard_map/all_to_all | solution.py:170
  193.5 17.4 %all-to-all-done = bf16[64,2,640]{2,1,0:T(2,128)(2,1)S(1)} async-done(((bf16[64,2,640]{2,1,0:T(2,128)(2,1)}), bf16[64,2,640]{2,1,0:T(2,128)(2,1)S(1)}, u32[]{:S(2)}, u32[]{:S(2)}) %all-to-all-start) | async-done | bytes 163872 | tf_op jit(solution)/shard_map/all_to_all | solution.py:170
  210.8 6.8 all-to-all-start.1
  220.8 22.2 %all-to-all-done.1 = bf16[64,2,640]{2,1,0:T(2,128)(2,1)S(1)} async-done(((bf16[64,2,640]{2,1,0:T(2,128)(2,1)}), bf16[64,2,640]{2,1,0:T(2,128)(2,1)S(1)}, u32[]{:S(2)}, u32[]{:S(2)}) %all-to-all-start.1) | async-done | bytes 163872 | tf_op jit(solution)/shard_map/all_to_all | solution.py:170
  242.9 4.6 all-to-all-start.2
  253.2 16.0 %all-to-all-done.2 = bf16[64,2,640]{2,1,0:T(2,128)(2,1)S(1)} async-done(((bf16[64,2,640]{2,1,0:T(2,128)(2,1)}), bf16[64,2,640]{2,1,0:T(2,128)(2,1)S(1)}, u32[]{:S(2)}, u32[]{:S(2)}) %all-to-all-start.2) | async-done | bytes 163872 | tf_op jit(solution)/shard_map/all_to_all | solution.py:170
  269.2 12.3 %all-to-all-start.3 = ((bf16[64,2,640]{2,1,0:T(2,128)(2,1)}), bf16[64,2,640]{2,1,0:T(2,128)(2,1)S(1)}, u32[]{:S(2)}, u32[]{:S(2)}) async-start(bf16[64,2,640]{2,1,0:T(2,128)(2,1)} %reshape.366), calls=%async_computation.4 | async-start | bytes 327680 | tf_op jit(solution)/shard_map/all_to_all | solution.py:170
  281.5 3.2 all-gather.8.cloned.1.call-done
  284.7 130.7 %all-gather.12.cloned.1.call-done = bf16[16384,1,1,80]{0,3,2,1:T(8,128)(2,1)} async-done(((bf16[256,1,1,80]{0,3,2,1:T(8,128)(2,1)}), bf16[16384,1,1,80]{0,3,2,1:T(8,128)(2,1)}) %all-gather.12.cloned.1.call-update) | async-done | bytes 2621456 | tf_op jit(solution)/shard_map/all_gather | solution.py:76
  415.5 64.7 %while.18 = (s32[]{:T(128)}, f32[1,1024]{1,0:T(1,128)S(1)}, f32[1,1024]{1,0:T(1,128)S(1)}, f32[1,1024,80]{1,2,0:T(8,128)S(1)}, s32[]{:T(128)}, /*index=5*/bf16[1...) while((s32[]{:T(128)}, f32[1,1024]{1,0:T(1,128)S(1)}, ...), condition=%wide.region_8.9_spmd.clone, body=%wide.region_2.8_spmd.clone.sunk | while | flops 176327680 | bytes 7374129 | solution.py:112
  417.3 3.8 conditional.3
  419.5 1.7 fusion.5
  480.2 137.3 %all-to-all-start.4 = ((bf16[64,2,640]{2,1,0:T(2,128)(2,1)}), bf16[64,2,640]{2,1,0:T(2,128)(2,1)S(1)}, u32[]{:S(2)}, u32[]{:S(2)}) async-start(bf16[64,2,640]{2,1,0:T(2,128)(2,1)} %reshape.368), calls=%async_computation.5 | async-start | bytes 327680 | tf_op jit(solution)/shard_map/all_to_all | solution.py:170
  617.8 3.4 convolution_convert_fusion
  623.6 12.6 %all-to-all-done.4 = bf16[64,2,640]{2,1,0:T(2,128)(2,1)S(1)} async-done(((bf16[64,2,640]{2,1,0:T(2,128)(2,1)}), bf16[64,2,640]{2,1,0:T(2,128)(2,1)S(1)}, u32[]{:S(2)}, u32[]{:S(2)}) %all-to-all-start.4) | async-done | bytes 163872 | tf_op jit(solution)/shard_map/all_to_all | solution.py:170
  636.3 5.1 all-to-all-start.5
  641.4 1.6 reduce.10
  643.7 18.5 %all-to-all-done.5 = bf16[64,2,640]{2,1,0:T(2,128)(2,1)S(1)} async-done(((bf16[64,2,640]{2,1,0:T(2,128)(2,1)}), bf16[64,2,640]{2,1,0:T(2,128)(2,1)S(1)}, u32[]{:S(2)}, u32[]{:S(2)}) %all-to-all-start.5) | async-done | bytes 163872 | tf_op jit(solution)/shard_map/all_to_all | solution.py:170
  662.2 4.6 all-to-all-start.6
  669.1 15.5 %all-to-all-done.6 = bf16[64,2,640]{2,1,0:T(2,128)(2,1)S(1)} async-done(((bf16[64,2,640]{2,1,0:T(2,128)(2,1)}), bf16[64,2,640]{2,1,0:T(2,128)(2,1)S(1)}, u32[]{:S(2)}, u32[]{:S(2)}) %all-to-all-start.6) | async-done | bytes 163872 | tf_op jit(solution)/shard_map/all_to_all | solution.py:170
  684.7 4.6 all-to-all-start.7
  690.1 2.0 sort.46
  692.1 2.0 sort.47
  695.8 11.7 %all-to-all-done.7 = bf16[64,2,640]{2,1,0:T(2,128)(2,1)S(1)} async-done(((bf16[64,2,640]{2,1,0:T(2,128)(2,1)}), bf16[64,2,640]{2,1,0:T(2,128)(2,1)S(1)}, u32[]{:S(2)}, u32[]{:S(2)}) %all-to-all-start.7) | async-done | bytes 163872 | tf_op jit(solution)/shard_map/all_to_all | solution.py:170
  708.3 6.6 stack.3
  (227 shorter events, 55.0 us)
Async XLA Ops:
  7.2 126.8 %all-gather.6.cloned.1.call-start = ((), (), s32[]{:S(2)}) async-start(), calls=%async_computation.9 | async-start | bytes 2662400 | tf_op jit(solution)/shard_map/all_gather | solution.py:40
  7.9 276.8 %all-gather.8.cloned.1.call-start = ((), (), s32[]{:S(2)}) async-start(), calls=%async_computation.10 | async-start | bytes 2662400 | tf_op jit(solution)/shard_map/all_gather | solution.py:75
  9.6 129.4 %copy-start.1 = (s32[4096]{0:T(1024)S(1)}, s32[4096]{0:T(1024)}, u32[]{:S(2)}) copy-start(s32[4096]{0:T(1024)} %param.20) | copy-start | bytes 49156
  9.7 145.0 %copy-start = (s32[4096]{0:T(1024)S(1)}, s32[4096]{0:T(1024)}, u32[]{:S(2)}) copy-start(s32[4096]{0:T(1024)} %param.21) | copy-start | bytes 49156
  9.7 160.7 %copy-start.3 = (s32[8]{0:T(128)S(1)}, s32[8]{0:T(128)}, u32[]{:S(2)}) copy-start(s32[8]{0:T(128)} %param.19) | copy-start | bytes 100
  137.4 36.4 %copy-start.2 = (bf16[8,64,1,1280]{3,1,2,0:T(8,128)(2,1)S(1)}, bf16[8,64,1,1280]{3,1,2,0:T(8,128)(2,1)}, u32[]{:S(2)}) copy-start(bf16[8,64,1,1280]{3,1,2,0:T(8,128)(2,1)} %param.18) | copy-start | bytes 3932164
  138.3 277.1 %all-gather.12.cloned.1.call-start = ((), (), s32[]{:S(2)}) async-start(), calls=%async_computation.13 | async-start | bytes 2662400 | tf_op jit(solution)/shard_map/all_gather | solution.py:76
  180.8 30.0 %all-to-all-start = ((bf16[64,2,640]{2,1,0:T(2,128)(2,1)}), bf16[64,2,640]{2,1,0:T(2,128)(2,1)S(1)}, u32[]{:S(2)}, u32[]{:S(2)}) async-start(bf16[64,2,640]{2,1,0:T(2,128)(2,1)} %reshape.360), calls=%async_computation.1 | async-start | bytes 327680 | tf_op jit(solution)/shard_map/all_to_all | solution.py:170
  210.8 32.1 %all-to-all-start.1 = ((bf16[64,2,640]{2,1,0:T(2,128)(2,1)}), bf16[64,2,640]{2,1,0:T(2,128)(2,1)S(1)}, u32[]{:S(2)}, u32[]{:S(2)}) async-start(bf16[64,2,640]{2,1,0:T(2,128)(2,1)} %reshape.362), calls=%async_computation.2 | async-start | bytes 327680 | tf_op jit(solution)/shard_map/all_to_all | solution.py:170
  217.6 400.2 %all-gather.10.cloned.1.call-start = ((), (), s32[]{:S(2)}) async-start(), calls=%async_computation.11 | async-start | bytes 1996800 | tf_op jit(solution)/shard_map/all_gather | solution.py:125
  242.9 26.2 %all-to-all-start.2 = ((bf16[64,2,640]{2,1,0:T(2,128)(2,1)}), bf16[64,2,640]{2,1,0:T(2,128)(2,1)S(1)}, u32[]{:S(2)}, u32[]{:S(2)}) async-start(bf16[64,2,640]{2,1,0:T(2,128)(2,1)} %reshape.364), calls=%async_computation.3 | async-start | bytes 327680 | tf_op jit(solution)/shard_map/all_to_all | solution.py:170
  269.2 211.0 %all-to-all-start.3 = ((bf16[64,2,640]{2,1,0:T(2,128)(2,1)}), bf16[64,2,640]{2,1,0:T(2,128)(2,1)S(1)}, u32[]{:S(2)}, u32[]{:S(2)}) async-start(bf16[64,2,640]{2,1,0:T(2,128)(2,1)} %reshape.366), calls=%async_computation.4 | async-start | bytes 327680 | tf_op jit(solution)/shard_map/all_to_all | solution.py:170
  480.2 156.0 %all-to-all-start.4 = ((bf16[64,2,640]{2,1,0:T(2,128)(2,1)}), bf16[64,2,640]{2,1,0:T(2,128)(2,1)S(1)}, u32[]{:S(2)}, u32[]{:S(2)}) async-start(bf16[64,2,640]{2,1,0:T(2,128)(2,1)} %reshape.368), calls=%async_computation.5 | async-start | bytes 327680 | tf_op jit(solution)/shard_map/all_to_all | solution.py:170
  617.6 99.5 %reduce-scatter.2.cloned.1.call-start = ((), (), s32[]{:S(2)}) async-start(), calls=%async_computation.12 | async-start | bytes 1474560 | tf_op jit(solution)/shard_map/reduce_scatter | solution.py:128
  636.3 25.9 %all-to-all-start.5 = ((bf16[64,2,640]{2,1,0:T(2,128)(2,1)}), bf16[64,2,640]{2,1,0:T(2,128)(2,1)S(1)}, u32[]{:S(2)}, u32[]{:S(2)}) async-start(bf16[64,2,640]{2,1,0:T(2,128)(2,1)} %reshape.370), calls=%async_computation.6 | async-start | bytes 327680 | tf_op jit(solution)/shard_map/all_to_all | solution.py:170
  662.2 22.5 %all-to-all-start.6 = ((bf16[64,2,640]{2,1,0:T(2,128)(2,1)}), bf16[64,2,640]{2,1,0:T(2,128)(2,1)S(1)}, u32[]{:S(2)}, u32[]{:S(2)}) async-start(bf16[64,2,640]{2,1,0:T(2,128)(2,1)} %reshape.372), calls=%async_computation.7 | async-start | bytes 327680 | tf_op jit(solution)/shard_map/all_to_all | solution.py:170
  684.7 22.8 %all-to-all-start.7 = ((bf16[64,2,640]{2,1,0:T(2,128)(2,1)}), bf16[64,2,640]{2,1,0:T(2,128)(2,1)S(1)}, u32[]{:S(2)}, u32[]{:S(2)}) async-start(bf16[64,2,640]{2,1,0:T(2,128)(2,1)} %reshape.374), calls=%async_computation.8 | async-start | bytes 327680 | tf_op jit(solution)/shard_map/all_to_all | solution.py:170
Sparse Core Ops, SparseCore 0:
  12.2 121.7 all-gather.5
  138.4 146.2 all-gather.7
  288.7 126.6 all-gather.11
  419.5 113.9 all-gather.9
  621.5 42.9 reduce-scatter.1
where the time goes:
time: 728 us; the launch traced here: 724 us
  waiting for transfers between devices  373 us (51%)
  starting transfers between devices  186 us (26%)
  local copies, waits for them, and re-layouts  54.5 us (7%)
  other arithmetic  46 us (6%)
  loops' own time  39.5 us (5%)
  between operations  14.3 us (2%)
  matrix products  9.9 us (1%)
    all_to_all x8, starting transfers between devices, hand_over(): lax.all_to_all(sending, 'tok', split_axis=0, concat_axis=0, tiled=True)  186 us
    all_gather x1, waiting for transfers between devices, attend(): value_part = lax.all_gather(values, 'tok', axis=0, tiled=True)  131 us
    all_gather x1, waiting for transfers between devices, attend(): lax.all_gather(w_qkv, 'tok', axis=0, tiled=True)  124 us
    all_to_all x8, waiting for transfers between devices, hand_over(): lax.all_to_all(sending, 'tok', split_axis=0, concat_axis=0, tiled=True)  114 us
    another operation x1, loops' own time, attend(): lax.fori_loop(0, row_count // step_rows, advance, initial)  38.6 us
    add x32, other arithmetic, key_positions(): whole_rows = block_start + jnp.arange(count, dtype=jnp.int32)  21.3 us
    scatter x1, local copies, waits for them, and re-layouts, hand_over(): jnp.zeros((block_total,), jnp.int32).at[decode_table].set(every_block)  15.5 us
    scatter x1, local copies, waits for them, and re-layouts, hand_over(): jnp.zeros((block_total,), jnp.int32).at[prefill_table].set(every_block)  15.5 us
  transfers between devices with their start and end apart: 13, of which 10 were waited for; matrix products, arithmetic and copies ran while one was open for 15% of the time, Pallas kernels for 0%

commit v1 on v0

v1 whole, which is shorter than its diff:
```python
import functools
import math

import jax
import jax.numpy as jnp
from jax import lax
from jax.experimental import pallas as pl
from jax.experimental.pallas import tpu as pltpu
from jax.sharding import PartitionSpec as P

HD = 80
QPK = 4
BLK = 8
LANES = 128
SIDE = 4

NORM_EPS = 1e-05
ROPE_BASE = 1000000.0
LOWEST = -1e30
EXP2_SCALE = math.log2(math.e) / math.sqrt(HD)

MESH = pl.DeviceIdType.MESH


def coordinates():
    index = lax.axis_index("tok")
    return index // 16, (index // 4) % 4, index % 4


def along(axis, step):
    place = list(coordinates())
    place[axis] = (place[axis] + step) % SIDE
    return (place[0] * SIDE + place[1]) * SIDE + place[2]


def greet(far):
    barrier = pltpu.get_barrier_semaphore()
    peers = [along(axis, step) for axis in range(3) for step in (1, 3)]
    peers += [along(axis, 2) for axis in far]
    for peer in peers:
        pl.semaphore_signal(barrier, inc=1, device_id={"tok": peer}, device_id_type=MESH)
    pl.semaphore_wait(barrier, len(peers))


def remote(src, dst, send_sem, recv_sem, peer):
    return pltpu.make_async_remote_copy(
        src_ref=src,
        dst_ref=dst,
        send_sem=send_sem,
        recv_sem=recv_sem,
        device_id={"tok": peer},
        device_id_type=MESH,
    )


ORDERS = ((0, 1, 2), (0, 2, 1))


class Gather:
    def __init__(self, src, buf, split, send_sem, recv_sem, own_sem):
        self.src, self.buf, self.split = src, buf, split
        self.send_sem, self.recv_sem, self.own_sem = send_sem, recv_sem, own_sem
        self.sent = []

    def own(self):
        z, y, x = coordinates()
        for part in range(2):
            pltpu.make_async_copy(
                self.src.at[part], self.buf.at[part, z, y, x], self.own_sem.at[part]
            ).start()
        for part in range(2):
            pltpu.make_async_copy(
                self.src.at[part], self.buf.at[part, z, y, x], self.own_sem.at[part]
            ).wait()

    def view(self, part, phase, step, rows):
        done = ORDERS[part][:phase]
        axis = ORDERS[part][phase]
        place = list(coordinates())
        place[axis] = (place[axis] + step) % SIDE
        for seen in done:
            place[seen] = slice(None)
        return self.buf.at[(part, *place, rows, slice(None))]

    def copy(self, part, phase, which):
        axis = ORDERS[part][phase]
        every = slice(None)
        upper, lower = pl.ds(0, self.split), pl.ds(self.split, self.buf.shape[4] - self.split)
        step, rows, way = (
            (0, every, 1),
            (0, every, 3),
            (3, upper, 1),
            (1, lower, 3),
        )[which]
        view = self.view(part, phase, step, rows)
        return remote(
            view,
            view,
            self.send_sem.at[part, phase, which],
            self.recv_sem.at[part, phase, which],
            along(axis, way),
        )

    def start(self, phase):
        for part in range(2):
            for which in (0, 1):
                self.copy(part, phase, which).start()

    def pass_on(self, phase):
        for part in range(2):
            for which in (0, 1):
                self.copy(part, phase, which).wait_recv()
                self.copy(part, phase, which + 2).start()

    def finish(self, phase):
        for part in range(2):
            for which in (2, 3):
                self.copy(part, phase, which).wait_recv()

    def drain(self):
        for part in range(2):
            for phase in range(3):
                for which in range(4):
                    self.copy(part, phase, which).wait_send()


class Exchange:
    def __init__(self, src, first, second, dst, relay, send_sem, recv_sem, own_sem):
        self.bufs = (src, first, second, dst)
        self.relay = relay
        self.send_sem, self.recv_sem, self.own_sem = send_sem, recv_sem, own_sem

    def part(self, phase, buf, index, half):
        place = [slice(None)] * 3
        if half is not None:
            place[1 if phase == 0 else 0] = pl.ds(2 * half, 2)
        place[phase] = index
        return buf.at[tuple(place)]

    def own(self, phase):
        here = coordinates()[phase]
        return pltpu.make_async_copy(
            self.part(phase, self.bufs[phase], here, None),
            self.part(phase, self.bufs[phase + 1], here, None),
            self.own_sem.at[phase],
        )

    def copy(self, phase, which):
        here = coordinates()[phase]
        src, dst = self.bufs[phase], self.bufs[phase + 1]
        sems = (self.send_sem.at[phase, which], self.recv_sem.at[phase, which])
        if which < 2:
            step = (1, 3)[which]
            there = (here + step) % SIDE
            return remote(
                self.part(phase, src, there, None),
                self.part(phase, dst, here, None),
                *sems,
                along(phase, step),
            )
        half = which % 2
        step = (1, 3)[half]
        relay = self.relay.at[phase, half]
        if which < 4:
            there = (here + 2) % SIDE
            return remote(self.part(phase, src, there, half), relay, *sems, along(phase, step))
        origin = (here + 4 - step) % SIDE
        return remote(relay, self.part(phase, dst, origin, half), *sems, along(phase, step))

    def start(self, phase):
        self.own(phase).start()
        for which in (2, 3, 0, 1):
            self.copy(phase, which).start()

    def pass_on(self, phase):
        for which in (2, 3):
            self.copy(phase, which).wait_recv()
            self.copy(phase, which + 2).start()

    def finish(self, phase):
        self.own(phase).wait()
        for which in (0, 1, 4, 5):
            self.copy(phase, which).wait_recv()

    def drain(self):
        for phase in range(3):
            for which in range(6):
                self.copy(phase, which).wait_send()


def gather_kernel(split, src, buf, send_sem, recv_sem, own_sem):
    greet(())
    gather = Gather(src, buf, split, send_sem, recv_sem, own_sem)
    gather.own()
    for phase in range(3):
        gather.start(phase)
        gather.pass_on(phase)
        gather.finish(phase)
    gather.drain()


def gather_sems():
    return [
        pltpu.SemaphoreType.DMA((2, 3, 4)),
        pltpu.SemaphoreType.DMA((2, 3, 4)),
        pltpu.SemaphoreType.DMA((2,)),
    ]


VMEM_SPEC = pl.BlockSpec(memory_space=pltpu.VMEM)


def gather_tok(block, split, collective_id):
    rows = block.shape[1]
    return pl.pallas_call(
        functools.partial(gather_kernel, split),
        out_shape=jax.ShapeDtypeStruct((2, SIDE, SIDE, SIDE, rows, LANES), block.dtype),
        in_specs=[VMEM_SPEC],
        out_specs=VMEM_SPEC,
        scratch_shapes=gather_sems(),
        compiler_params=pltpu.CompilerParams(
            collective_id=collective_id, has_side_effects=True
        ),
        name="gather_tok",
    )(block)


def move_kernel(
    kv_src,
    out_src,
    cache_src,
    kv_buf,
    out_buf,
    cache_dst,
    first,
    second,
    relay,
    kv_send,
    kv_recv,
    kv_own,
    out_send,
    out_recv,
    out_own,
    cache_send,
    cache_recv,
    cache_own,
):
    greet(())
    kv = Gather(kv_src, kv_buf, HD, kv_send, kv_recv, kv_own)
    out = Gather(out_src, out_buf, 32, out_send, out_recv, out_own)
    cache = Exchange(cache_src, first, second, cache_dst, relay, cache_send, cache_recv, cache_own)
    kv.own()
    kv.start(0)
    out.own()
    kv.pass_on(0)
    kv.finish(0)
    kv.start(1)
    cache.start(0)
    kv.pass_on(1)
    kv.finish(1)
    kv.start(2)
    out.start(0)
    kv.pass_on(2)
    kv.finish(2)
    out.pass_on(0)
    cache.pass_on(0)
    out.finish(0)
    out.start(1)
    out.pass_on(1)
    out.finish(1)
    out.start(2)
    out.pass_on(2)
    out.finish(2)
    cache.finish(0)
    for phase in (1, 2):
        cache.start(phase)
        cache.pass_on(phase)
        cache.finish(phase)
    kv.drain()
    out.drain()
    cache.drain()


def move(kv_block, out_block, cache_block):
    def gathered(block):
        return jax.ShapeDtypeStruct((2, SIDE, SIDE, SIDE, block.shape[1], LANES), block.dtype)

    unit = cache_block.shape[3:]
    kind = cache_block.dtype
    return pl.pallas_call(
        move_kernel,
        out_shape=(
            gathered(kv_block),
            gathered(out_block),
            jax.ShapeDtypeStruct(cache_block.shape, kind),
        ),
        in_specs=[VMEM_SPEC] * 3,
        out_specs=[VMEM_SPEC] * 3,
        scratch_shapes=[
            pltpu.VMEM(cache_block.shape, kind),
            pltpu.VMEM(cache_block.shape, kind),
            pltpu.VMEM((3, 2, 2, SIDE, *unit), kind),
            *gather_sems(),
            *gather_sems(),
            pltpu.SemaphoreType.DMA((3, 6)),
            pltpu.SemaphoreType.DMA((3, 6)),
            pltpu.SemaphoreType.DMA((3,)),
        ],
        compiler_params=pltpu.CompilerParams(collective_id=1, has_side_effects=True),
        name="move",
    )(kv_block, out_block, cache_block)


def attend_group(group, masked, query, kv, top, total, weighted):
    z, y = group // SIDE, group % SIDE
    blocks = [(x, part) for x in range(SIDE) for part in range(2)]
    key = jnp.concatenate([kv[part, z, y, x, :HD, :] for x, part in blocks], axis=1)
    value = jnp.concatenate([kv[part, z, y, x, HD:, :] for x, part in blocks], axis=1)
    count = key.shape[1]
    width = query.shape[1] // QPK
    for head in range(QPK):
        cols = pl.ds(head * width, width)
        score = lax.dot_general(
            key, query[:, cols], (((0,), (0,)), ((), ())), preferred_element_type=jnp.float32
        )
        if masked:
            limit = coordinates()[2] * width
            rows = lax.broadcasted_iota(jnp.int32, (count, width), 0)
            lanes = lax.broadcasted_iota(jnp.int32, (count, width), 1)
            score = jnp.where(rows <= lanes + limit, score, LOWEST)
        before = top[:, cols]
        highest = jnp.maximum(before, jnp.max(score, axis=0, keepdims=True))
        expo = jnp.exp2((score - highest) * EXP2_SCALE)
        shrink = jnp.exp2((before - highest) * EXP2_SCALE)
        total[:, cols] = total[:, cols] * shrink + jnp.sum(expo, axis=0, keepdims=True)
        weighted[:, cols] = weighted[:, cols] * shrink + jnp.dot(
            value, expo.astype(jnp.bfloat16), preferred_element_type=jnp.float32
        )
        top[:, cols] = highest


def attend_kernel(query, kv, context, top, total, weighted):
    top[...] = jnp.full_like(top, LOWEST)
    total[...] = jnp.zeros_like(total)
    weighted[...] = jnp.zeros_like(weighted)
    last = lax.axis_index("tok") // SIDE

    def step(group, carry):
        attend_group(group, False, query, kv, top, total, weighted)
        return carry

    lax.fori_loop(0, last, step, 0)
    attend_group(last, True, query, kv, top, total, weighted)
    context[...] = (weighted[...] / total[...]).astype(context.dtype)


def attend(query, kv):
    columns = query.shape[1]
    return pl.pallas_call(
        attend_kernel,
        out_shape=jax.ShapeDtypeStruct((HD, columns), jnp.bfloat16),
        in_specs=[VMEM_SPEC] * 2,
        out_specs=VMEM_SPEC,
        scratch_shapes=[
            pltpu.VMEM((1, columns), jnp.float32),
            pltpu.VMEM((1, columns), jnp.float32),
            pltpu.VMEM((HD, columns), jnp.float32),
        ],
        name="attend",
    )(query, kv)


def pack_weight(block, lane_chunks, rows):
    height, width = block.shape
    block = jnp.pad(block, ((0, 0), (0, lane_chunks * LANES - width)))
    block = block.reshape(height, lane_chunks, LANES).transpose(1, 0, 2)
    block = block.reshape(lane_chunks * height, LANES)
    block = jnp.pad(block, ((0, 2 * rows - lane_chunks * height), (0, 0)))
    return block.reshape(2, rows, LANES)


def unpack_weight(buf, lane_chunks, height, width):
    rows = buf.shape[4]
    count = SIDE * SIDE * SIDE
    buf = buf.reshape(2, count, rows, LANES).transpose(1, 0, 2, 3)
    buf = buf.reshape(count, 2 * rows, LANES)[:, : lane_chunks * height]
    buf = buf.reshape(count, lane_chunks, height, LANES).transpose(0, 2, 1, 3)
    return buf.reshape(count * height, lane_chunks * LANES)[:, :width]


def project(hidden_in, norm_gain, weight):
    tok_rows = hidden_in.shape[0]
    float_rows = hidden_in.astype(jnp.float32)
    normed = (
        float_rows
        * lax.rsqrt(jnp.mean(float_rows * float_rows, axis=-1, keepdims=True) + NORM_EPS)
        * norm_gain
    ).astype(jnp.bfloat16)
    projected = lax.dot_general(
        weight, normed, (((0,), (1,)), ((), ())), preferred_element_type=jnp.float32
    ).reshape(QPK + 2, HD, tok_rows)
    half = HD // 2
    frequency = ROPE_BASE ** (-2.0 * jnp.arange(half, dtype=jnp.float32) / HD)
    positions = lax.axis_index("tok") * tok_rows + jnp.arange(tok_rows, dtype=jnp.int32)
    angles = frequency[:, None] * positions.astype(jnp.float32)[None, :]
    cosine, sines = jnp.cos(angles)[None], jnp.sin(angles)[None]
    front, back = projected[: QPK + 1, :half], projected[: QPK + 1, half:]
    turned = jnp.concatenate(
        [front * cosine - back * sines, back * cosine + front * sines], axis=1
    ).astype(jnp.bfloat16)
    query = turned[:QPK].transpose(1, 0, 2).reshape(HD, QPK * tok_rows)
    key_value = jnp.concatenate([turned[QPK], projected[QPK + 1].astype(jnp.bfloat16)], axis=0)
    key_value = key_value.reshape(2 * HD, 2, LANES).transpose(1, 0, 2)
    return query, key_value


def outgoing_blocks(prefill_cache, lengths, prefill_table, decode_table):
    tok_count = lax.axis_size("tok")
    my_index = lax.axis_index("tok")
    layers, slot_count, _, extent = prefill_cache.shape
    block_total = prefill_table.shape[0]
    per_request = block_total // lengths.shape[0]
    every_block = jnp.arange(block_total, dtype=jnp.int32)
    slots = jnp.arange(slot_count, dtype=jnp.int32)
    mine = prefill_table[:, None] == (my_index * slot_count + slots)[None, :]
    held_here = jnp.sum(jnp.where(mine, every_block[:, None], 0), axis=0)
    target = jnp.sum(jnp.where(mine, (decode_table // slot_count)[:, None], 0), axis=0)
    request = held_here // per_request
    requests = jnp.arange(lengths.shape[0], dtype=jnp.int32)
    request_len = jnp.sum(
        jnp.where(request[:, None] == requests[None, :], lengths[None, :], 0), axis=1
    )
    first_token = held_here % per_request * BLK
    live = first_token[:, None] + jnp.arange(BLK, dtype=jnp.int32)[None, :] < request_len[:, None]
    peers = jnp.arange(tok_count, dtype=jnp.int32)
    slot_of = jnp.sum(jnp.where(target[None, :] == peers[:, None], slots[None, :], 0), axis=1)
    origin = (my_index - (target - my_index)) % tok_count
    blocks = prefill_cache.reshape(layers, slot_count, BLK, extent // BLK)
    blocks = jnp.where(live[None, :, :, None], blocks, jnp.zeros_like(blocks))
    blocks = blocks.reshape(layers, slot_count, extent).transpose(1, 0, 2)
    blocks = jnp.take(blocks, slot_of, axis=0)
    blocks = blocks.reshape(SIDE, SIDE, SIDE, layers * extent // LANES, LANES)
    return blocks, origin


def on_device(
    hidden_in, norm_gain, w_qkv, w_out, prefill_cache, lengths, prefill_table, decode_table
):
    tok_rows = hidden_in.shape[0]
    layers, slot_count, kv_local, extent = prefill_cache.shape
    gathered = gather_tok(pack_weight(w_qkv, 4, 80), 48, 0)
    weight = unpack_weight(gathered, 4, *w_qkv.shape)
    query, key_value = project(hidden_in, norm_gain, weight)
    blocks, origin = outgoing_blocks(prefill_cache, lengths, prefill_table, decode_table)
    kv_all, out_all, arrived = move(key_value, pack_weight(w_out.T, 3, 64), blocks)
    context = attend(query, kv_all)
    context = context.reshape(HD, QPK, tok_rows).transpose(2, 1, 0).reshape(tok_rows, QPK * HD)
    out_weight = unpack_weight(out_all, 3, w_out.shape[1], w_out.shape[0])
    partial = lax.dot_general(
        context, out_weight, (((1,), (1,)), ((), ())), preferred_element_type=jnp.float32
    )
    attn_out = lax.psum_scatter(
        partial.astype(jnp.bfloat16), "head", scatter_dimension=1, tiled=True
    )
    arrived = arrived.reshape(slot_count, layers, extent)
    decode_cache = jnp.take(arrived, origin, axis=0).transpose(1, 0, 2)
    return attn_out, decode_cache.reshape(prefill_cache.shape)


def solution(mesh):
    in_specs = (
        P("tok", None),
        P(),
        P("tok", "head"),
        P("head", "tok"),
        P(None, "tok", "head", None),
        P(),
        P(),
        P(),
    )
    out_specs = (P("tok", "head"), P(None, "tok", "head", None))
    return jax.shard_map(
        on_device, mesh=mesh, in_specs=in_specs, out_specs=out_specs, check_vma=False
    )
```

time: 728 us -> 300 us (0.41)
  the two profiles are of different devices: /device:TPU:64 before, /device:TPU:14 now
where the time goes in v1:
time: 300 us; the launch traced here: 299 us
  Pallas kernels  183 us (61%)
  waiting for transfers between devices  76 us (25%)
  local copies, waits for them, and re-layouts  18.5 us (6%)
  between operations  14.4 us (5%)
  matrix products  4.16 us (1%)
  other arithmetic  3.37 us (1%)
    pallas_call x1, Pallas kernels, move(): pl.pallas_call(move_kernel, out_shape=(gathered(kv_block), gathered(out_b...  126 us
    reduce_scatter x1, waiting for transfers between devices, on_device(): lax.psum_scatter(partial.astype(jnp.bfloat16), 'head', scatter_dimension=...  76 us
    pallas_call x1, Pallas kernels, gather_tok(): pl.pallas_call(functools.partial(gather_kernel, split), out_shape=jax.Sha...  47.8 us
    pallas_call x1, Pallas kernels, attend(): pl.pallas_call(attend_kernel, out_shape=jax.ShapeDtypeStruct((HD, columns...  9.38 us
  transfers between devices with their start and end apart: 1, of which 1 were waited for; matrix products, arithmetic and copies ran while one was open for 1% of the time, Pallas kernels for 0%

profile of v1, /device:TPU:14, one launch (start us, length us, event | category | flops | bytes accessed | tf_op | source)
XLA Modules:
  0.0 299.4 jit_solution(4112963896150565100)
XLA Ops:
  7.2 1.4 copy_bitcast_fusion.4
  8.6 47.8 %gather_tok.1 = bf16[2,4,4,4,80,128]{5,4,3,2,1,0:T(8,128)(2,1)} custom-call(bf16[2,80,128]{2,1,0:T(8,128)(2,1)} %bitcast.80), custom_call_target="tpu_custom_call" | custom-call | tf_op jit(solution)/shard_map/gather_tok/pallas_call | solution.py:215
  56.4 1.9 copy.39
  58.4 1.0 copy.40
  59.4 0.5 copy.62
  59.9 0.8 copy-done.1
  60.7 0.3 fusion
  61.1 0.3 copy-done.7
  61.4 2.2 fusion.3
  63.8 0.2 multiply_cosine_fusion
  64.1 0.3 copy-done.5
  64.5 0.4 fusion.11
  65.0 0.7 copy.53
  65.8 0.6 pad.14
  66.7 0.3 broadcast_in_dim.91
  67.0 1.0 fusion.7
  68.0 0.6 gather_fusion
  68.6 0.2 broadcast_select_fusion
  68.8 2.4 reshape.239.cache_src
  71.2 0.6 maximum_bitcast_fusion.kv_src
  71.8 125.7 %move.1 = (bf16[2,4,4,4,160,128]{5,4,3,2,1,0:T(8,128)(2,1)}, bf16[2,4,4,4,64,128]{5,4,3,2,1,0:T(8,128)(2,1)}, bf16[4,4,4,80,128]{4,3,2,1,0:T(8,128)(2,1)}) custom-call(bf16[2,160,128]{2,1,0:T(8,128)(2,1)} %maximum_bitcast_fusion.kv_src, bf16[2,64,128]{2,1,0:T(8,128)(2,1)} %bitcast.81, bf16[4,4,4,80,128]{4,3,2,1,0:T(8,128)(2,1)} %reshape.239.cache_src), custom_call_target="tpu_custom_call" | custom-call | tf_op jit(solution)/shard_map/move/pallas_call | solution.py:290
  197.6 9.4 %attend.1 = bf16[80,1024]{1,0:T(8,128)(2,1)} custom-call(bf16[80,1024]{1,0:T(8,128)(2,1)} %bitcast.75, bf16[2,4,4,4,160,128]{5,4,3,2,1,0:T(8,128)(2,1)} %get-tuple-element.6.kv), custom_call_target="tpu_custom_call" | custom-call | tf_op jit(solution)/shard_map/attend/pallas_call | solution.py:359
  207.0 0.9 copy.64
  208.2 1.0 copy.48
  209.3 0.3 copy.63
  209.6 1.9 convolution_convert_fusion
  211.6 1.3 copy-done.3
  212.9 1.5 reshape.246
  214.5 0.6 gather_fusion.1
  215.1 0.2 select_bitcast_fusion
  215.3 1.3 copy.49
  216.6 76.0 %reduce-scatter.2.cloned.1.call-done = bf16[256,320]{0,1:T(8,128)(2,1)} async-done(((bf16[256,2560]{0,1:T(8,128)(2,1)}), bf16[256,320]{0,1:T(8,128)(2,1)}) %reduce-scatter.2.cloned.1.call-update) | async-done | bytes 163856 | tf_op jit(solution)/shard_map/reduce_scatter | solution.py:462
  (42 shorter events, 1.1 us)
Async XLA Ops:
  7.2 285.4 %reduce-scatter.2.cloned.1.call-start = ((), (), s32[]{:S(2)}) async-start(), calls=%async_computation.1 | async-start | bytes 1474560 | tf_op jit(solution)/shard_map/reduce_scatter | solution.py:462
  59.4 1.3 copy-start.1
  60.7 0.7 copy-start.7
  63.7 0.7 copy-start.5
  63.7 0.7 copy-start.6
  63.7 2.0 copy-start.4
  63.7 2.7 copy-start.8
  63.8 3.3 %copy-start.2 = (bf16[8,64,1,1280]{3,1,2,0:T(8,128)(2,1)S(1)}, bf16[8,64,1,1280]{3,1,2,0:T(8,128)(2,1)}, u32[]{:S(2)}) copy-start(bf16[8,64,1,1280]{3,1,2,0:T(8,128)(2,1)} %param.14) | copy-start | bytes 3932164
  197.6 10.3 %copy-start = (bf16[2,4,4,4,64,128]{5,4,3,2,1,0:T(8,128)(2,1)S(1)}, bf16[2,4,4,4,64,128]{5,4,3,2,1,0:T(8,128)(2,1)}, u32[]{:S(2)}) copy-start(bf16[2,4,4,4,64,128]{5,4,3,2,1,0:T(8,128)(2,1)} %get-tuple-element.7) | copy-start | bytes 6291460
  211.6 1.3 copy-start.3
Sparse Core Ops, SparseCore 0:
  211.7 80.8 reduce-scatter.1

commit v2 on v1

--- a/solution.py
+++ b/solution.py
@@ -125,20 +125,20 @@
 
 
 class Exchange:
-    def __init__(self, src, first, second, dst, relay, send_sem, recv_sem, own_sem):
-        self.bufs = (src, first, second, dst)
-        self.relay = relay
+    def __init__(self, order, phases, bufs, relay, send_sem, recv_sem, own_sem):
+        self.order, self.phases, self.bufs, self.relay = order, phases, bufs, relay
         self.send_sem, self.recv_sem, self.own_sem = send_sem, recv_sem, own_sem
 
     def part(self, phase, buf, index, half):
+        axis = self.order[phase]
         place = [slice(None)] * 3
         if half is not None:
-            place[1 if phase == 0 else 0] = pl.ds(2 * half, 2)
-        place[phase] = index
+            place[1 if axis == 0 else 0] = pl.ds(2 * half, 2)
+        place[axis] = index
         return buf.at[tuple(place)]
 
     def own(self, phase):
-        here = coordinates()[phase]
+        here = coordinates()[self.order[phase]]
         return pltpu.make_async_copy(
             self.part(phase, self.bufs[phase], here, None),
             self.part(phase, self.bufs[phase + 1], here, None),
@@ -146,7 +146,8 @@
         )
 
     def copy(self, phase, which):
-        here = coordinates()[phase]
+        axis = self.order[phase]
+        here = coordinates()[axis]
         src, dst = self.bufs[phase], self.bufs[phase + 1]
         sems = (self.send_sem.at[phase, which], self.recv_sem.at[phase, which])
         if which < 2:
@@ -156,16 +157,16 @@
                 self.part(phase, src, there, None),
                 self.part(phase, dst, here, None),
                 *sems,
-                along(phase, step),
+                along(axis, step),
             )
         half = which % 2
         step = (1, 3)[half]
-        relay = self.relay.at[phase, half]
+        relay = self.relay.at[phase - self.phases[0], half]
         if which < 4:
             there = (here + 2) % SIDE
-            return remote(self.part(phase, src, there, half), relay, *sems, along(phase, step))
+            return remote(self.part(phase, src, there, half), relay, *sems, along(axis, step))
         origin = (here + 4 - step) % SIDE
-        return remote(relay, self.part(phase, dst, origin, half), *sems, along(phase, step))
+        return remote(relay, self.part(phase, dst, origin, half), *sems, along(axis, step))
 
     def start(self, phase):
         self.own(phase).start()
@@ -183,20 +184,45 @@
             self.copy(phase, which).wait_recv()
 
     def drain(self):
-        for phase in range(3):
+        for phase in self.phases:
             for which in range(6):
                 self.copy(phase, which).wait_send()
 
 
-def gather_kernel(split, src, buf, send_sem, recv_sem, own_sem):
+def relay_buffer(block, phases):
+    return pltpu.VMEM((phases, 2, 2, SIDE, *block.shape[3:]), block.dtype)
+
+
+def gather_kernel(
+    split,
+    src,
+    cache_src,
+    buf,
+    cache_dst,
+    relay,
+    send_sem,
+    recv_sem,
+    own_sem,
+    cache_send,
+    cache_recv,
+    cache_own,
+):
     greet(())
     gather = Gather(src, buf, split, send_sem, recv_sem, own_sem)
+    cache = Exchange(
+        ORDERS[0], (0,), (cache_src, cache_dst), relay, cache_send, cache_recv, cache_own
+    )
     gather.own()
     for phase in range(3):
         gather.start(phase)
         gather.pass_on(phase)
+        if phase == 0:
+            cache.start(0)
         gather.finish(phase)
+    cache.pass_on(0)
+    cache.finish(0)
     gather.drain()
+    cache.drain()
 
 
 def gather_sems():
@@ -207,127 +233,67 @@
     ]
 
 
+def exchange_sems():
+    return [
+        pltpu.SemaphoreType.DMA((3, 6)),
+        pltpu.SemaphoreType.DMA((3, 6)),
+        pltpu.SemaphoreType.DMA((3,)),
+    ]
+
+
 VMEM_SPEC = pl.BlockSpec(memory_space=pltpu.VMEM)
 
 
-def gather_tok(block, split, collective_id):
-    rows = block.shape[1]
+def like(block):
+    return jax.ShapeDtypeStruct(block.shape, block.dtype)
+
+
+def gathered(block):
+    return jax.ShapeDtypeStruct((2, SIDE, SIDE, SIDE, block.shape[1], LANES), block.dtype)
+
+
+def gather_tok(block, cache_block, split):
     return pl.pallas_call(
         functools.partial(gather_kernel, split),
-        out_shape=jax.ShapeDtypeStruct((2, SIDE, SIDE, SIDE, rows, LANES), block.dtype),
-        in_specs=[VMEM_SPEC],
-        out_specs=VMEM_SPEC,
-        scratch_shapes=gather_sems(),
-        compiler_params=pltpu.CompilerParams(
-            collective_id=collective_id, has_side_effects=True
-        ),
+        out_shape=(gathered(block), like(cache_block)),
+        in_specs=[VMEM_SPEC] * 2,
+        out_specs=[VMEM_SPEC] * 2,
+        scratch_shapes=[relay_buffer(cache_block, 1), *gather_sems(), *exchange_sems()],
+        compiler_params=pltpu.CompilerParams(collective_id=0, has_side_effects=True),
         name="gather_tok",
-    )(block)
-
-
-def move_kernel(
-    kv_src,
-    out_src,
-    cache_src,
-    kv_buf,
-    out_buf,
-    cache_dst,
-    first,
-    second,
-    relay,
-    kv_send,
-    kv_recv,
-    kv_own,
-    out_send,
-    out_recv,
-    out_own,
-    cache_send,
-    cache_recv,
-    cache_own,
-):
-    greet(())
-    kv = Gather(kv_src, kv_buf, HD, kv_send, kv_recv, kv_own)
-    out = Gather(out_src, out_buf, 32, out_send, out_recv, out_own)
-    cache = Exchange(cache_src, first, second, cache_dst, relay, cache_send, cache_recv, cache_own)
-    kv.own()
-    kv.start(0)
-    out.own()
-    kv.pass_on(0)
-    kv.finish(0)
-    kv.start(1)
-    cache.start(0)
-    kv.pass_on(1)
-    kv.finish(1)
-    kv.start(2)
-    out.start(0)
-    kv.pass_on(2)
-    kv.finish(2)
-    out.pass_on(0)
-    cache.pass_on(0)
-    out.finish(0)
-    out.start(1)
-    out.pass_on(1)
-    out.finish(1)
-    out.start(2)
-    out.pass_on(2)
-    out.finish(2)
-    cache.finish(0)
-    for phase in (1, 2):
-        cache.start(phase)
-        cache.pass_on(phase)
-        cache.finish(phase)
-    kv.drain()
-    out.drain()
-    cache.drain()
-
-
-def move(kv_block, out_block, cache_block):
-    def gathered(block):
-        return jax.ShapeDtypeStruct((2, SIDE, SIDE, SIDE, block.shape[1], LANES), block.dtype)
-
-    unit = cache_block.shape[3:]
-    kind = cache_block.dtype
-    return pl.pallas_call(
-        move_kernel,
-        out_shape=(
-            gathered(kv_block),
-            gathered(out_block),
-            jax.ShapeDtypeStruct(cache_block.shape, kind),
-        ),
-        in_specs=[VMEM_SPEC] * 3,
-        out_specs=[VMEM_SPEC] * 3,
-        scratch_shapes=[
-            pltpu.VMEM(cache_block.shape, kind),
-            pltpu.VMEM(cache_block.shape, kind),
-            pltpu.VMEM((3, 2, 2, SIDE, *unit), kind),
-            *gather_sems(),
-            *gather_sems(),
-            pltpu.SemaphoreType.DMA((3, 6)),
-            pltpu.SemaphoreType.DMA((3, 6)),
-            pltpu.SemaphoreType.DMA((3,)),
-        ],
-        compiler_params=pltpu.CompilerParams(collective_id=1, has_side_effects=True),
-        name="move",
-    )(kv_block, out_block, cache_block)
-
-
-def attend_group(group, masked, query, kv, top, total, weighted):
-    z, y = group // SIDE, group % SIDE
-    blocks = [(x, part) for x in range(SIDE) for part in range(2)]
-    key = jnp.concatenate([kv[part, z, y, x, :HD, :] for x, part in blocks], axis=1)
-    value = jnp.concatenate([kv[part, z, y, x, HD:, :] for x, part in blocks], axis=1)
-    count = key.shape[1]
+    )(block, cache_block)
+
+
+def attend_group(z, k, masked, query, kv, top, total, weighted):
+    my_z, my_y, my_x = coordinates()
+    x, y = (my_x + k) % SIDE, (my_y + k) % SIDE
+    places = [(0, other, x) for other in range(SIDE)] + [(1, y, other) for other in range(SIDE)]
+    key = jnp.concatenate([kv[part, z, v, u, :HD, :] for part, v, u in places], axis=1)
+    value = jnp.concatenate([kv[part, z, v, u, HD:, :] for part, v, u in places], axis=1)
     width = query.shape[1] // QPK
+    if masked:
+        shape = (LANES, width)
+        ahead = lax.broadcasted_iota(jnp.int32, shape, 0) - lax.broadcasted_iota(
+            jnp.int32, shape, 1
+        )
+        behind = [
+            ((my_y - v) * SIDE + my_x - u) * width - part * LANES for part, v, u in places
+        ]
     for head in range(QPK):
         cols = pl.ds(head * width, width)
         score = lax.dot_general(
             key, query[:, cols], (((0,), (0,)), ((), ())), preferred_element_type=jnp.float32
         )
         if masked:
-            limit = coordinates()[2] * width
-            rows = lax.broadcasted_iota(jnp.int32, (count, width), 0)
-            lanes = lax.broadcasted_iota(jnp.int32, (count, width), 1)
-            score = jnp.where(rows <= lanes + limit, score, LOWEST)
+            score = jnp.concatenate(
+                [
+                    jnp.where(
+                        ahead <= limit, score[place * LANES : (place + 1) * LANES], LOWEST
+                    )
+                    for place, limit in enumerate(behind)
+                ],
+                axis=0,
+            )
         before = top[:, cols]
         highest = jnp.maximum(before, jnp.max(score, axis=0, keepdims=True))
         expo = jnp.exp2((score - highest) * EXP2_SCALE)
@@ -339,35 +305,215 @@
         top[:, cols] = highest
 
 
-def attend_kernel(query, kv, context, top, total, weighted):
+def attend_kernel(
+    query,
+    kv_src,
+    out_src,
+    first_a,
+    cache_b,
+    context,
+    out_buf,
+    cache_dst_a,
+    cache_dst_b,
+    kv_buf,
+    second_a,
+    first_b,
+    second_b,
+    relay_a,
+    relay_b,
+    top,
+    total,
+    weighted,
+    *sems,
+):
+    greet(())
+    kv = Gather(kv_src, kv_buf, HD, *sems[0:3])
+    out = Gather(out_src, out_buf, 32, *sems[3:6])
+    half_a = Exchange(
+        ORDERS[0], (1, 2), (None, first_a, second_a, cache_dst_a), relay_a, *sems[6:9]
+    )
+    half_b = Exchange(
+        ORDERS[1], (0, 1, 2), (cache_b, first_b, second_b, cache_dst_b), relay_b, *sems[9:12]
+    )
+    my_z = coordinates()[0]
+
+    def earlier_rows(k):
+        def step(z, carry):
+            attend_group(z, k, False, query, kv_buf, top, total, weighted)
+            return carry
+
+        lax.fori_loop(0, my_z, step, 0)
+
+    def own_row(low, high):
+        def step(k, carry):
+            attend_group(my_z, k, True, query, kv_buf, top, total, weighted)
+            return carry
+
+        lax.fori_loop(low, high, step, 0)
+
+    kv.own()
+    kv.start(0)
+    out.own()
     top[...] = jnp.full_like(top, LOWEST)
     total[...] = jnp.zeros_like(total)
     weighted[...] = jnp.zeros_like(weighted)
-    last = lax.axis_index("tok") // SIDE
-
-    def step(group, carry):
-        attend_group(group, False, query, kv, top, total, weighted)
-        return carry
-
-    lax.fori_loop(0, last, step, 0)
-    attend_group(last, True, query, kv, top, total, weighted)
-    context[...] = (weighted[...] / total[...]).astype(context.dtype)
-
-
-def attend(query, kv):
+    kv.pass_on(0)
+    half_b.start(0)
+    kv.finish(0)
+    kv.start(1)
+    kv.pass_on(1)
+    kv.finish(1)
+    kv.start(2)
+    out.start(0)
+    own_row(0, 1)
+    earlier_rows(0)
+    kv.pass_on(2)
+    out.pass_on(0)
+    half_b.pass_on(0)
+    earlier_rows(1)
+    out.finish(0)
+    out.start(1)
+    half_b.finish(0)
+    half_a.start(1)
+    half_b.start(1)
+    earlier_rows(3)
+    kv.finish(2)
+    half_a.pass_on(1)
+    half_b.pass_on(1)
+    out.pass_on(1)
+    earlier_rows(2)
+    half_a.finish(1)
+    half_a.start(2)
+    half_b.finish(1)
+    half_b.start(2)
+    out.finish(1)
+    out.start(2)
+    own_row(1, 4)
+    half_a.pass_on(2)
+    half_b.pass_on(2)
+    out.pass_on(2)
+    width = query.shape[1] // QPK
+    for head in range(QPK):
+        cols = pl.ds(head * width, width)
+        context[pl.ds(head * HD, HD), :] = (weighted[:, cols] / total[:, cols]).astype(
+            context.dtype
+        )
+    half_a.finish(2)
+    half_b.finish(2)
+    out.finish(2)
+    kv.drain()
+    out.drain()
+    half_a.drain()
+    half_b.drain()
+
+
+def attend(query, kv_block, out_block, first_a, cache_b):
     columns = query.shape[1]
+    cache = pltpu.VMEM(cache_b.shape, cache_b.dtype)
     return pl.pallas_call(
         attend_kernel,
-        out_shape=jax.ShapeDtypeStruct((HD, columns), jnp.bfloat16),
-        in_specs=[VMEM_SPEC] * 2,
-        out_specs=VMEM_SPEC,
+        out_shape=(
+            jax.ShapeDtypeStruct((QPK * HD, columns // QPK), jnp.bfloat16),
+            gathered(out_block),
+            like(first_a),
+            like(cache_b),
+        ),
+        in_specs=[VMEM_SPEC] * 5,
+        out_specs=[VMEM_SPEC] * 4,
         scratch_shapes=[
+            pltpu.VMEM(gathered(kv_block).shape, kv_block.dtype),
+            cache,
+            cache,
+            cache,
+            relay_buffer(first_a, 2),
+            relay_buffer(cache_b, 3),
             pltpu.VMEM((1, columns), jnp.float32),
             pltpu.VMEM((1, columns), jnp.float32),
             pltpu.VMEM((HD, columns), jnp.float32),
+            *gather_sems(),
+            *gather_sems(),
+            *exchange_sems(),
+            *exchange_sems(),
         ],
+        compiler_params=pltpu.CompilerParams(collective_id=1, has_side_effects=True),
         name="attend",
-    )(query, kv)
+    )(query, kv_block, out_block, first_a, cache_b)
+
+
+def head_sum_kernel(part, result, swapped, pair, arrived, swap_sem, send_sem, recv_sem):
+    index = lax.axis_index("head")
+    chip, core = index // 2, index % 2
+    partner = chip * 2 + 1 - core
+    others = [((chip + step) % SIDE) * 2 + core for step in (1, 2, 3)]
+    barrier = pltpu.get_barrier_semaphore()
+    for peer in (partner, *others):
+        pl.semaphore_signal(barrier, inc=1, device_id={"head": peer}, device_id_type=MESH)
+    pl.semaphore_wait(barrier, 4)
+
+    def to_partner(step):
+        return pltpu.make_async_remote_copy(
+            src_ref=part.at[(chip + step) % SIDE, 1 - core],
+            dst_ref=swapped.at[step],
+            send_sem=swap_sem.at[0, step],
+            recv_sem=swap_sem.at[1, step],
+            device_id={"head": partner},
+            device_id_type=MESH,
+        )
+
+    def to_chip(step):
+        return pltpu.make_async_remote_copy(
+            src_ref=pair.at[step],
+            dst_ref=arrived.at[step],
+            send_sem=send_sem.at[step],
+            recv_sem=recv_sem.at[step],
+            device_id={"head": others[step - 1]},
+            device_id_type=MESH,
+        )
+
+    def add(step):
+        mine = part[(chip + step) % SIDE, core].astype(jnp.float32)
+        return mine + swapped[step].astype(jnp.float32)
+
+    order = (2, 1, 3)
+    for step in (*order, 0):
+        to_partner(step).start()
+    for place, step in enumerate(order):
+        to_partner(step).wait_recv()
+        pair[step] = add(step).astype(pair.dtype)
+        if place:
+            to_chip(order[place - 1]).start()
+    to_partner(0).wait_recv()
+    pair[0] = add(0).astype(pair.dtype)
+    to_chip(order[-1]).start()
+    whole = pair[0].astype(jnp.float32)
+    for step in (1, 3, 2):
+        to_chip(step).wait_recv()
+        whole = whole + arrived[step].astype(jnp.float32)
+    result[...] = whole.astype(result.dtype)
+    for step in order:
+        to_chip(step).wait_send()
+    for step in range(SIDE):
+        to_partner(step).wait_send()
+
+
+def head_sum(part):
+    slices = pltpu.VMEM((SIDE, *part.shape[2:]), part.dtype)
+    return pl.pallas_call(
+        head_sum_kernel,
+        out_shape=jax.ShapeDtypeStruct(part.shape[2:], part.dtype),
+        in_specs=[VMEM_SPEC],
+        out_specs=VMEM_SPEC,
+        scratch_shapes=[
+            slices,
+            slices,
+            slices,
+            pltpu.SemaphoreType.DMA((2, SIDE)),
+            pltpu.SemaphoreType.DMA((SIDE,)),
+            pltpu.SemaphoreType.DMA((SIDE,)),
+        ],
+        compiler_params=pltpu.CompilerParams(collective_id=2, has_side_effects=True),
+        name="head_sum",
+    )(part)
 
 
 def pack_weight(block, lane_chunks, rows):
@@ -439,30 +585,34 @@
     blocks = jnp.where(live[None, :, :, None], blocks, jnp.zeros_like(blocks))
     blocks = blocks.reshape(layers, slot_count, extent).transpose(1, 0, 2)
     blocks = jnp.take(blocks, slot_of, axis=0)
-    blocks = blocks.reshape(SIDE, SIDE, SIDE, layers * extent // LANES, LANES)
-    return blocks, origin
+    near = layers // 2
+    halves = [
+        half.reshape(SIDE, SIDE, SIDE, near * extent // LANES, LANES)
+        for half in (blocks[:, :near], blocks[:, near:])
+    ]
+    return halves, origin
 
 
 def on_device(
     hidden_in, norm_gain, w_qkv, w_out, prefill_cache, lengths, prefill_table, decode_table
 ):
-    tok_rows = hidden_in.shape[0]
     layers, slot_count, kv_local, extent = prefill_cache.shape
-    gathered = gather_tok(pack_weight(w_qkv, 4, 80), 48, 0)
-    weight = unpack_weight(gathered, 4, *w_qkv.shape)
-    query, key_value = project(hidden_in, norm_gain, weight)
-    blocks, origin = outgoing_blocks(prefill_cache, lengths, prefill_table, decode_table)
-    kv_all, out_all, arrived = move(key_value, pack_weight(w_out.T, 3, 64), blocks)
-    context = attend(query, kv_all)
-    context = context.reshape(HD, QPK, tok_rows).transpose(2, 1, 0).reshape(tok_rows, QPK * HD)
+    (cache_a, cache_b), origin = outgoing_blocks(
+        prefill_cache, lengths, prefill_table, decode_table
+    )
+    weights, first_a = gather_tok(pack_weight(w_qkv, 4, 80), cache_a, 48)
+    query, key_value = project(hidden_in, norm_gain, unpack_weight(weights, 4, *w_qkv.shape))
+    context, out_all, *arrived = attend(
+        query, key_value, pack_weight(w_out.T, 3, 64), first_a, cache_b
+    )
     out_weight = unpack_weight(out_all, 3, w_out.shape[1], w_out.shape[0])
-    partial = lax.dot_general(
-        context, out_weight, (((1,), (1,)), ((), ())), preferred_element_type=jnp.float32
-    )
-    attn_out = lax.psum_scatter(
-        partial.astype(jnp.bfloat16), "head", scatter_dimension=1, tiled=True
-    )
-    arrived = arrived.reshape(slot_count, layers, extent)
+    part = jnp.dot(out_weight, context, preferred_element_type=jnp.float32).astype(jnp.bfloat16)
+    heads = lax.axis_size("head")
+    part = part.reshape(heads // 2, 2, part.shape[0] // heads, part.shape[1])
+    attn_out = head_sum(part).T
+    arrived = jnp.concatenate(
+        [half.reshape(slot_count, layers // 2, extent) for half in arrived], axis=1
+    )
     decode_cache = jnp.take(arrived, origin, axis=0).transpose(1, 0, 2)
     return attn_out, decode_cache.reshape(prefill_cache.shape)
 

time: 300 us -> 207 us (0.69)
  the two profiles are of different devices: /device:TPU:14 before, /device:TPU:449 now
where the time goes in v2:
time: 207 us; the launch traced here: 206 us
  Pallas kernels  176 us (85%)
  local copies, waits for them, and re-layouts  18.4 us (9%)
  other arithmetic  7.35 us (4%)
  matrix products  2.86 us (1%)
    pallas_call x1, Pallas kernels, attend(): pl.pallas_call(attend_kernel, out_shape=(jax.ShapeDtypeStruct((QPK * HD,...  92.3 us
    pallas_call x1, Pallas kernels, gather_tok(): pl.pallas_call(functools.partial(gather_kernel, split), out_shape=(gather...  44.7 us
    pallas_call x1, Pallas kernels, head_sum(): pl.pallas_call(head_sum_kernel, out_shape=jax.ShapeDtypeStruct(part.shape...  39.3 us
    unnamed x18, local copies, waits for them, and re-layouts  5.87 us

profile of v2, /device:TPU:449, one launch (start us, length us, event | category | flops | bytes accessed | tf_op | source)
XLA Modules:
  0.0 205.9 jit_solution(14667023672559676638)
XLA Ops:
  0.6 0.7 add_select_fusion
  1.4 1.1 fusion.11
  2.5 0.7 select_reduce_fusion.1
  3.4 0.3 broadcast_in_dim.91
  3.7 2.3 %fusion.7 = bf16[64,8,1280]{2,1,0:T(8,128)(2,1)S(1)} fusion(bf16[8,64,1,1280]{3,1,2,0:T(8,128)(2,1)} %param.14, pred[64,1280]{1,0:T(8,128)(4,1)S(1)} %broadcast_in_dim.91), kind=kLoop, calls=%fused_computation.17 | loop fusion | flops 655360 | bytes 2703360 | tf_op jit(solution)/shard_map/transpose | solution.py:586
  6.1 0.6 gather_fusion
  7.0 0.4 fusion.19
  7.4 1.1 reshape.235.cache_src
  8.5 0.6 copy_bitcast_fusion.3
  9.1 44.7 %gather_tok.1 = (bf16[2,4,4,4,80,128]{5,4,3,2,1,0:T(8,128)(2,1)}, bf16[4,4,4,40,128]{4,3,2,1,0:T(8,128)(2,1)}) custom-call(bf16[2,80,128]{2,1,0:T(8,128)(2,1)} %bitcast.77, bf16[4,4,4,40,128]{4,3,2,1,0:T(8,128)(2,1)} %reshape.235.cache_src), custom_call_target="tpu_custom_call" | custom-call | tf_op jit(solution)/shard_map/gather_tok/pallas_call | solution.py:256
  53.9 1.9 copy.39
  55.8 1.0 copy.40
  56.9 0.5 copy.58
  57.3 0.8 copy-done.1
  58.2 0.3 fusion
  58.5 0.9 fusion.3
  59.9 0.6 maximum_bitcast_fusion.kv_src
  60.5 0.7 copy.50
  61.2 1.1 reshape.243.cache_b
  62.3 0.6 pad.14
  62.9 92.3 %attend.1 = (bf16[320,256]{1,0:T(8,128)(2,1)}, bf16[2,4,4,4,64,128]{5,4,3,2,1,0:T(8,128)(2,1)}, bf16[4,4,4,40,128]{4,3,2,1,0:T(8,128)(2,1)}, bf16[4,4,4,40,128]{4,3,2,1,0:T(8,128)(2,1)}) custom-call(bf16[80,1024]{1,0:T(8,128)(2,1)} %bitcast.73, bf16[2,160,128]{2,1,0:T(8,128)(2,1)} %maximum_bitcast_fusion.kv_src, bf16[2,64,128]{2,1,0:T(8,128)(2,1)} %bitcast.78, ...), custom_call_target="tpu_custom_call" | custom-call | tf_op jit(solution)/shard_map/attend/pallas_call | solution.py:413
  155.3 1.7 reshape.249
  157.2 0.6 pad_maximum_fusion
  157.9 0.6 gather_fusion.1
  158.8 1.3 copy.47
  160.0 0.8 copy-done
  161.2 1.0 copy.46
  162.3 0.3 copy.59
  162.6 0.6 copy-done.5
  163.2 1.9 convolution_convert_fusion
  165.1 39.3 %head_sum.1 = bf16[320,256]{1,0:T(8,128)(2,1)} custom-call(bf16[4,2,320,256]{3,2,1,0:T(8,128)(2,1)} %bitcast.72), custom_call_target="tpu_custom_call" | custom-call | tf_op jit(solution)/shard_map/head_sum/pallas_call | solution.py:501
  204.4 1.6 copy.61
  (39 shorter events, 1.8 us)
Async XLA Ops:
  7.4 1.1 copy-start.3
  56.9 1.3 copy-start.1
  57.3 1.2 copy-start.6
  59.8 2.5 %copy-start.4 = (bf16[320,40]{0,1:T(8,128)(2,1)S(1)}, bf16[320,40]{0,1:T(8,128)(2,1)}, u32[]{:S(2)}) copy-start(bf16[320,40]{0,1:T(8,128)(2,1)} %param.13) | copy-start | bytes 76804
  155.3 1.7 copy-start.2
  158.7 2.1 %copy-start = (bf16[2,4,4,4,64,128]{5,4,3,2,1,0:T(8,128)(2,1)S(1)}, bf16[2,4,4,4,64,128]{5,4,3,2,1,0:T(8,128)(2,1)}, u32[]{:S(2)}) copy-start(bf16[2,4,4,4,64,128]{5,4,3,2,1,0:T(8,128)(2,1)} %get-tuple-element.11) | copy-start | bytes 6291460
  162.3 0.9 copy-start.5

commit v3 on v2

--- a/solution.py
+++ b/solution.py
@@ -12,6 +12,7 @@
 QPK = 4
 BLK = 8
 LANES = 128
+NEAR = 3 * LANES
 SIDE = 4
 
 NORM_EPS = 1e-05
@@ -122,6 +123,99 @@
             for phase in range(3):
                 for which in range(4):
                     self.copy(part, phase, which).wait_send()
+
+
+class Flow:
+    def __init__(self, src, buf, split, z_send, z_recv, send_sem, recv_sem, own_sem):
+        self.src, self.buf, self.split = src, buf, split
+        self.z_send, self.z_recv = z_send, z_recv
+        self.send_sem, self.recv_sem, self.own_sem = send_sem, recv_sem, own_sem
+
+    def own(self):
+        z, y, x = coordinates()
+        copy = pltpu.make_async_copy(self.src, self.buf.at[:, z, y, x], self.own_sem)
+        copy.start()
+        copy.wait()
+
+    def plan(self, which):
+        upper, lower = pl.ds(0, self.split), pl.ds(self.split, self.buf.shape[4] - self.split)
+        every = slice(None)
+        return ((0, every, 1), (0, every, 3), (3, upper, 1), (1, lower, 3))[which]
+
+    def z_copy(self, which):
+        step, rows, way = self.plan(which)
+        z, y, x = coordinates()
+        view = self.buf.at[:, (z + step) % SIDE, y, x, rows, :]
+        return remote(view, view, self.z_send.at[which], self.z_recv.at[which], along(0, way))
+
+    def z_start(self):
+        self.z_copy(0).start()
+        self.z_copy(1).start()
+
+    def z_pass_on(self):
+        for which in (0, 1):
+            self.z_copy(which).wait_recv()
+            self.z_copy(which + 2).start()
+
+    def z_finish(self):
+        for which in (2, 3):
+            self.z_copy(which).wait_recv()
+
+    def copy(self, row, part, phase, which):
+        step, rows, way = self.plan(which)
+        axis = ORDERS[part][1 + phase]
+        place = list(coordinates())
+        place[0] = (place[0] + row) % SIDE
+        place[axis] = (place[axis] + step) % SIDE
+        if phase:
+            place[ORDERS[part][1]] = slice(None)
+        view = self.buf.at[(part, *place, rows, slice(None))]
+        sem = (row, part, phase, which)
+        return remote(view, view, self.send_sem.at[sem], self.recv_sem.at[sem], along(axis, way))
+
+    def start(self, row, phase):
+        for part in range(2):
+            for which in (0, 1):
+                self.copy(row, part, phase, which).start()
+
+    def pass_on(self, row, phase):
+        for part in range(2):
+            for which in (0, 1):
+                self.copy(row, part, phase, which).wait_recv()
+                self.copy(row, part, phase, which + 2).start()
+
+    def finish(self, row, phase):
+        for part in range(2):
+            for which in (2, 3):
+                self.copy(row, part, phase, which).wait_recv()
+
+    def drain(self):
+        for which in range(4):
+            self.z_copy(which).wait_send()
+        for row in range(SIDE):
+            for part in range(2):
+                for phase in range(2):
+                    for which in range(4):
+                        self.copy(row, part, phase, which).wait_send()
+
+    def head(self, beside):
+        self.own()
+        self.z_start()
+        self.start(0, 0)
+        self.pass_on(0, 0)
+        self.finish(0, 0)
+        self.start(0, 1)
+        self.z_pass_on()
+        beside()
+        self.start(3, 0)
+        self.start(1, 0)
+        self.pass_on(0, 1)
+        for row in (3, 1):
+            self.pass_on(row, 0)
+        for row in (3, 1):
+            self.finish(row, 0)
+            self.start(row, 1)
+        self.finish(0, 1)
 
 
 class Exchange:
@@ -193,36 +287,36 @@
     return pltpu.VMEM((phases, 2, 2, SIDE, *block.shape[3:]), block.dtype)
 
 
-def gather_kernel(
-    split,
-    src,
-    cache_src,
-    buf,
-    cache_dst,
-    relay,
-    send_sem,
-    recv_sem,
-    own_sem,
-    cache_send,
-    cache_recv,
-    cache_own,
-):
+def gather_kernel(split, src, cache_src, buf, cache_dst, relay, *sems):
     greet(())
-    gather = Gather(src, buf, split, send_sem, recv_sem, own_sem)
-    cache = Exchange(
-        ORDERS[0], (0,), (cache_src, cache_dst), relay, cache_send, cache_recv, cache_own
-    )
-    gather.own()
-    for phase in range(3):
-        gather.start(phase)
-        gather.pass_on(phase)
-        if phase == 0:
-            cache.start(0)
-        gather.finish(phase)
+    gather = Flow(src, buf, split, *sems[0:5])
+    cache = Exchange(ORDERS[0], (0,), (cache_src, cache_dst), relay, *sems[5:8])
+    gather.head(lambda: cache.start(0))
+    gather.z_finish()
+    gather.start(2, 0)
+    for row in (3, 1):
+        gather.pass_on(row, 1)
+    gather.pass_on(2, 0)
+    gather.finish(2, 0)
+    gather.start(2, 1)
+    for row in (3, 1):
+        gather.finish(row, 1)
+    gather.pass_on(2, 1)
     cache.pass_on(0)
+    gather.finish(2, 1)
     cache.finish(0)
     gather.drain()
     cache.drain()
+
+
+def flow_sems():
+    return [
+        pltpu.SemaphoreType.DMA((4,)),
+        pltpu.SemaphoreType.DMA((4,)),
+        pltpu.SemaphoreType.DMA((SIDE, 2, 2, 4)),
+        pltpu.SemaphoreType.DMA((SIDE, 2, 2, 4)),
+        pltpu.SemaphoreType.DMA,
+    ]
 
 
 def gather_sems():
@@ -258,27 +352,24 @@
         out_shape=(gathered(block), like(cache_block)),
         in_specs=[VMEM_SPEC] * 2,
         out_specs=[VMEM_SPEC] * 2,
-        scratch_shapes=[relay_buffer(cache_block, 1), *gather_sems(), *exchange_sems()],
+        scratch_shapes=[relay_buffer(cache_block, 1), *flow_sems(), *exchange_sems()],
         compiler_params=pltpu.CompilerParams(collective_id=0, has_side_effects=True),
         name="gather_tok",
     )(block, cache_block)
 
 
-def attend_group(z, k, masked, query, kv, top, total, weighted):
-    my_z, my_y, my_x = coordinates()
-    x, y = (my_x + k) % SIDE, (my_y + k) % SIDE
-    places = [(0, other, x) for other in range(SIDE)] + [(1, y, other) for other in range(SIDE)]
-    key = jnp.concatenate([kv[part, z, v, u, :HD, :] for part, v, u in places], axis=1)
-    value = jnp.concatenate([kv[part, z, v, u, HD:, :] for part, v, u in places], axis=1)
+def attend_group(z, y, masked, query, kv, top, total, weighted):
+    places = [(part, x) for x in range(SIDE) for part in range(2)]
+    key = jnp.concatenate([kv[part, z, y, x, :HD, :] for part, x in places], axis=1)
+    value = jnp.concatenate([kv[part, z, y, x, HD:, :] for part, x in places], axis=1)
     width = query.shape[1] // QPK
     if masked:
         shape = (LANES, width)
         ahead = lax.broadcasted_iota(jnp.int32, shape, 0) - lax.broadcasted_iota(
             jnp.int32, shape, 1
         )
-        behind = [
-            ((my_y - v) * SIDE + my_x - u) * width - part * LANES for part, v, u in places
-        ]
+        my_x = coordinates()[2]
+        behind = [(my_x - x) * width - part * LANES for part, x in places]
     for head in range(QPK):
         cols = pl.ds(head * width, width)
         score = lax.dot_general(
@@ -327,71 +418,73 @@
     *sems,
 ):
     greet(())
-    kv = Gather(kv_src, kv_buf, HD, *sems[0:3])
-    out = Gather(out_src, out_buf, 32, *sems[3:6])
+    kv = Flow(kv_src, kv_buf, HD, *sems[0:5])
+    out = Gather(out_src, out_buf, 32, *sems[5:8])
     half_a = Exchange(
-        ORDERS[0], (1, 2), (None, first_a, second_a, cache_dst_a), relay_a, *sems[6:9]
+        ORDERS[0], (1, 2), (None, first_a, second_a, cache_dst_a), relay_a, *sems[8:11]
     )
     half_b = Exchange(
-        ORDERS[1], (0, 1, 2), (cache_b, first_b, second_b, cache_dst_b), relay_b, *sems[9:12]
+        ORDERS[1], (0, 1, 2), (cache_b, first_b, second_b, cache_dst_b), relay_b, *sems[11:14]
     )
-    my_z = coordinates()[0]
-
-    def earlier_rows(k):
-        def step(z, carry):
-            attend_group(z, k, False, query, kv_buf, top, total, weighted)
+    my_z, my_y, _ = coordinates()
+    state = (query, kv_buf, top, total, weighted)
+
+    def groups(z, low, count):
+        def step(y, carry):
+            attend_group(z, y, False, *state)
             return carry
 
-        lax.fori_loop(0, my_z, step, 0)
-
-    def own_row(low, high):
-        def step(k, carry):
-            attend_group(my_z, k, True, query, kv_buf, top, total, weighted)
-            return carry
-
-        lax.fori_loop(low, high, step, 0)
-
-    kv.own()
-    kv.start(0)
-    out.own()
+        lax.fori_loop(low, low + count, step, 0)
+
+    def row(step, half):
+        earlier = my_z // (SIDE - step)
+        earlier = jnp.minimum(earlier, 1)
+        groups((my_z + step) % SIDE, 2 * half, 2 * earlier)
+
     top[...] = jnp.full_like(top, LOWEST)
     total[...] = jnp.zeros_like(total)
     weighted[...] = jnp.zeros_like(weighted)
-    kv.pass_on(0)
-    half_b.start(0)
-    kv.finish(0)
-    kv.start(1)
-    kv.pass_on(1)
-    kv.finish(1)
-    kv.start(2)
+    kv.head(lambda: half_b.start(0))
+    out.own()
+    attend_group(my_z, my_y, True, *state)
+    kv.z_finish()
+    kv.start(2, 0)
     out.start(0)
-    own_row(0, 1)
-    earlier_rows(0)
-    kv.pass_on(2)
+    groups(my_z, 0, my_y)
+    for way in (3, 1):
+        kv.pass_on(way, 1)
+    kv.pass_on(2, 0)
+    kv.finish(2, 0)
+    kv.start(2, 1)
+    half_a.start(1)
     out.pass_on(0)
+    kv.finish(3, 1)
+    row(3, 0)
+    kv.pass_on(2, 1)
     half_b.pass_on(0)
-    earlier_rows(1)
+    half_a.pass_on(1)
     out.finish(0)
     out.start(1)
-    half_b.finish(0)
-    half_a.start(1)
-    half_b.start(1)
-    earlier_rows(3)
-    kv.finish(2)
-    half_a.pass_on(1)
-    half_b.pass_on(1)
+    row(3, 1)
+    kv.finish(1, 1)
+    kv.finish(2, 1)
     out.pass_on(1)
-    earlier_rows(2)
     half_a.finish(1)
     half_a.start(2)
+    row(1, 0)
+    half_b.finish(0)
+    half_b.start(1)
+    half_a.pass_on(2)
+    out.finish(1)
+    out.start(2)
+    row(1, 1)
+    half_b.pass_on(1)
+    out.pass_on(2)
+    row(2, 0)
     half_b.finish(1)
     half_b.start(2)
-    out.finish(1)
-    out.start(2)
-    own_row(1, 4)
-    half_a.pass_on(2)
+    row(2, 1)
     half_b.pass_on(2)
-    out.pass_on(2)
     width = query.shape[1] // QPK
     for head in range(QPK):
         cols = pl.ds(head * width, width)
@@ -422,7 +515,7 @@
         out_specs=[VMEM_SPEC] * 4,
         scratch_shapes=[
             pltpu.VMEM(gathered(kv_block).shape, kv_block.dtype),
-            cache,
+            pltpu.VMEM(first_a.shape, first_a.dtype),
             cache,
             cache,
             relay_buffer(first_a, 2),
@@ -430,7 +523,7 @@
             pltpu.VMEM((1, columns), jnp.float32),
             pltpu.VMEM((1, columns), jnp.float32),
             pltpu.VMEM((HD, columns), jnp.float32),
-            *gather_sems(),
+            *flow_sems(),
             *gather_sems(),
             *exchange_sems(),
             *exchange_sems(),
@@ -585,12 +678,8 @@
     blocks = jnp.where(live[None, :, :, None], blocks, jnp.zeros_like(blocks))
     blocks = blocks.reshape(layers, slot_count, extent).transpose(1, 0, 2)
     blocks = jnp.take(blocks, slot_of, axis=0)
-    near = layers // 2
-    halves = [
-        half.reshape(SIDE, SIDE, SIDE, near * extent // LANES, LANES)
-        for half in (blocks[:, :near], blocks[:, near:])
-    ]
-    return halves, origin
+    blocks = blocks.reshape(SIDE, SIDE, SIDE, layers, extent)
+    return (blocks[..., :NEAR], blocks[..., NEAR:]), origin
 
 
 def on_device(
@@ -610,9 +699,7 @@
     heads = lax.axis_size("head")
     part = part.reshape(heads // 2, 2, part.shape[0] // heads, part.shape[1])
     attn_out = head_sum(part).T
-    arrived = jnp.concatenate(
-        [half.reshape(slot_count, layers // 2, extent) for half in arrived], axis=1
-    )
+    arrived = jnp.concatenate(arrived, axis=-1).reshape(slot_count, layers, extent)
     decode_cache = jnp.take(arrived, origin, axis=0).transpose(1, 0, 2)
     return attn_out, decode_cache.reshape(prefill_cache.shape)
 

time: 207 us -> 205 us (level)
  Pallas kernels: 176 us -> 180 us
  local copies, waits for them, and re-layouts: 18.4 us -> 15.6 us
  other arithmetic: 7.35 us -> 4.94 us
    pallas_call x1, Pallas kernels: 92.3 us -> 103 us  [attend(): pl.pallas_call(attend_kernel, out_shape=(jax.ShapeDtypeStruct((QPK * HD,...]
    pallas_call x1, Pallas kernels: 44.7 us -> 38.5 us  [gather_tok(): pl.pallas_call(functools.partial(gather_kernel, split), out_shape=(gather...]
    reshape x4 -> x0, local copies, waits for them, and re-layouts: 4.09 us -> none  [the longest x2 2.16 us: outgoing_blocks(): half.reshape(SIDE, SIDE, SIDE, near * extent // LANES, LANES)]
    unnamed x18 -> x28, local copies, waits for them, and re-layouts: 5.87 us -> 4.18 us
where the time goes in v3:
time: 205 us; the launch traced here: 204 us
  Pallas kernels  180 us (88%)
  local copies, waits for them, and re-layouts  15.6 us (8%)
  other arithmetic  4.94 us (2%)
  matrix products  2.83 us (1%)
    pallas_call x1, Pallas kernels, attend(): pl.pallas_call(attend_kernel, out_shape=(jax.ShapeDtypeStruct((QPK * HD,...  103 us
    pallas_call x1, Pallas kernels, gather_tok(): pl.pallas_call(functools.partial(gather_kernel, split), out_shape=(gather...  38.5 us
    pallas_call x1, Pallas kernels, head_sum(): pl.pallas_call(head_sum_kernel, out_shape=jax.ShapeDtypeStruct(part.shape...  38.2 us
    unnamed x28, local copies, waits for them, and re-layouts  4.18 us

profile of v3, /device:TPU:449, one launch (start us, length us, event | category | flops | bytes accessed | tf_op | source)
XLA Modules:
  0.0 204.4 jit_solution(5036877770445045385)
XLA Ops:
  0.7 1.7 fusion
  2.5 0.4 fusion.11
  3.4 0.6 pad.14
  4.0 0.6 copy_bitcast_fusion.3
  4.6 0.2 multiply_cosine_fusion
  5.0 0.3 broadcast_in_dim.91
  5.3 1.0 fusion.7
  6.2 0.6 gather_fusion
  6.9 0.2 broadcast_select_fusion
  7.1 0.8 slice.46.cache_src
  7.9 1.0 slice.53.cache_b
  8.9 38.5 %gather_tok.1 = (bf16[2,4,4,4,80,128]{5,4,3,2,1,0:T(8,128)(2,1)}, bf16[4,4,4,8,384]{4,3,2,1,0:T(8,128)(2,1)}) custom-call(bf16[2,80,128]{2,1,0:T(8,128)(2,1)} %bitcast.78, bf16[4,4,4,8,384]{4,3,2,1,0:T(8,128)(2,1)} %slice.46.cache_src), custom_call_target="tpu_custom_call" | custom-call | tf_op jit(solution)/shard_map/gather_tok/pallas_call | solution.py:350
  47.4 1.9 copy.38
  49.3 1.0 copy.39
  50.4 0.5 copy.57
  50.8 0.8 copy-done.1
  51.7 0.9 fusion.3
  52.7 0.7 copy.49
  53.4 0.6 maximum_bitcast_fusion.kv_src
  54.1 103.3 %attend.1 = (bf16[320,256]{1,0:T(8,128)(2,1)}, bf16[2,4,4,4,64,128]{5,4,3,2,1,0:T(8,128)(2,1)}, bf16[4,4,4,8,384]{4,3,2,1,0:T(8,128)(2,1)}, bf16[4,4,4,8,896]{4,3,2,1,0:T(8,128)(2,1)}) custom-call(bf16[80,1024]{1,0:T(8,128)(2,1)} %bitcast.74, bf16[2,160,128]{2,1,0:T(8,128)(2,1)} %maximum_bitcast_fusion.kv_src, bf16[2,64,128]{2,1,0:T(8,128)(2,1)} %bitcast.79, ...), custom_call_target="tpu_custom_call" | custom-call | tf_op jit(solution)/shard_map/attend/pallas_call | solution.py:506
  157.4 1.8 copy.44
  159.2 0.2 slice.54
  159.4 1.0 copy.45
  160.4 0.3 copy.58
  160.8 0.6 copy-done.9
  161.3 1.9 convolution_convert_fusion
  163.2 38.2 %head_sum.1 = bf16[320,256]{1,0:T(8,128)(2,1)} custom-call(bf16[4,2,320,256]{3,2,1,0:T(8,128)(2,1)} %bitcast.73), custom_call_target="tpu_custom_call" | custom-call | tf_op jit(solution)/shard_map/head_sum/pallas_call | solution.py:594
  201.4 0.2 pad_maximum_fusion
  201.6 0.6 gather_fusion.1
  202.2 0.2 select_bitcast_fusion
  202.4 1.3 copy.46
  203.7 0.7 copy.60
  (46 shorter events, 0.7 us)
Async XLA Ops:
  0.6 1.9 copy-start.7
  0.6 1.9 copy-start.8
  0.7 2.5 %copy-start.11 = (s32[8]{0:T(128)S(1)}, s32[8]{0:T(128)}, u32[]{:S(2)}) copy-start(s32[8]{0:T(128)} %param.15) | copy-start | bytes 100
  0.7 4.6 %copy-start = (bf16[8,64,1,1280]{3,1,2,0:T(8,128)(2,1)S(1)}, bf16[8,64,1,1280]{3,1,2,0:T(8,128)(2,1)}, u32[]{:S(2)}) copy-start(bf16[8,64,1,1280]{3,1,2,0:T(8,128)(2,1)} %param.14) | copy-start | bytes 3932164
  0.7 2.6 %copy-start.6 = (bf16[320,40]{0,1:T(8,128)(2,1)S(1)}, bf16[320,40]{0,1:T(8,128)(2,1)}, u32[]{:S(2)}) copy-start(bf16[320,40]{0,1:T(8,128)(2,1)} %param.13) | copy-start | bytes 76804
  0.7 3.3 %copy-start.5 = (bf16[40,480]{1,0:T(8,128)(2,1)S(1)}, bf16[40,480]{1,0:T(8,128)(2,1)}, u32[]{:S(2)}) copy-start(bf16[40,480]{1,0:T(8,128)(2,1)} %param.12) | copy-start | bytes 115204
  50.3 1.3 copy-start.1
  50.4 1.3 copy-start.10
  160.4 0.9 copy-start.9
  163.2 38.2 %copy-start.2 = (bf16[4,4,4,8,896]{4,3,2,1,0:T(8,128)(2,1)S(1)}, bf16[4,4,4,8,896]{4,3,2,1,0:T(8,128)(2,1)}, u32[]{:S(2)}) copy-start(bf16[4,4,4,8,896]{4,3,2,1,0:T(8,128)(2,1)} %get-tuple-element.14) | copy-start | bytes 2752516
  163.2 38.2 %copy-start.4 = (bf16[4,4,4,8,384]{4,3,2,1,0:T(8,128)(2,1)S(1)}, bf16[4,4,4,8,384]{4,3,2,1,0:T(8,128)(2,1)}, u32[]{:S(2)}) copy-start(bf16[4,4,4,8,384]{4,3,2,1,0:T(8,128)(2,1)} %get-tuple-element.13) | copy-start | bytes 1179652
  202.4 1.3 copy-start.3

commit v4 on v3

--- a/solution.py
+++ b/solution.py
@@ -12,7 +12,7 @@
 QPK = 4
 BLK = 8
 LANES = 128
-NEAR = 3 * LANES
+NEAR = 4 * LANES
 SIDE = 4
 
 NORM_EPS = 1e-05
@@ -55,6 +55,7 @@
 
 
 ORDERS = ((0, 1, 2), (0, 2, 1))
+FAR_ORDER = (1, 2, 0)
 
 
 class Gather:
@@ -287,26 +288,40 @@
     return pltpu.VMEM((phases, 2, 2, SIDE, *block.shape[3:]), block.dtype)
 
 
-def gather_kernel(split, src, cache_src, buf, cache_dst, relay, *sems):
+def gather_kernel(
+    split, src, near_src, far_src, buf, near_dst, far_dst, far_first, near_relay, far_relay, *sems
+):
     greet(())
     gather = Flow(src, buf, split, *sems[0:5])
-    cache = Exchange(ORDERS[0], (0,), (cache_src, cache_dst), relay, *sems[5:8])
-    gather.head(lambda: cache.start(0))
+    near = Exchange(ORDERS[0], (0,), (near_src, near_dst), near_relay, *sems[5:8])
+    far = Exchange(FAR_ORDER, (0, 1), (far_src, far_first, far_dst), far_relay, *sems[8:11])
+
+    def beside():
+        near.start(0)
+        far.start(0)
+
+    gather.head(beside)
     gather.z_finish()
     gather.start(2, 0)
     for row in (3, 1):
         gather.pass_on(row, 1)
+    far.pass_on(0)
     gather.pass_on(2, 0)
     gather.finish(2, 0)
     gather.start(2, 1)
     for row in (3, 1):
         gather.finish(row, 1)
+    far.finish(0)
+    far.start(1)
     gather.pass_on(2, 1)
-    cache.pass_on(0)
+    near.pass_on(0)
+    far.pass_on(1)
     gather.finish(2, 1)
-    cache.finish(0)
+    near.finish(0)
+    far.finish(1)
     gather.drain()
-    cache.drain()
+    near.drain()
+    far.drain()
 
 
 def flow_sems():
@@ -346,16 +361,23 @@
     return jax.ShapeDtypeStruct((2, SIDE, SIDE, SIDE, block.shape[1], LANES), block.dtype)
 
 
-def gather_tok(block, cache_block, split):
+def gather_tok(block, near, far, split):
     return pl.pallas_call(
         functools.partial(gather_kernel, split),
-        out_shape=(gathered(block), like(cache_block)),
-        in_specs=[VMEM_SPEC] * 2,
-        out_specs=[VMEM_SPEC] * 2,
-        scratch_shapes=[relay_buffer(cache_block, 1), *flow_sems(), *exchange_sems()],
+        out_shape=(gathered(block), like(near), like(far)),
+        in_specs=[VMEM_SPEC] * 3,
+        out_specs=[VMEM_SPEC] * 3,
+        scratch_shapes=[
+            pltpu.VMEM(far.shape, far.dtype),
+            relay_buffer(near, 1),
+            relay_buffer(far, 2),
+            *flow_sems(),
+            *exchange_sems(),
+            *exchange_sems(),
+        ],
         compiler_params=pltpu.CompilerParams(collective_id=0, has_side_effects=True),
         name="gather_tok",
-    )(block, cache_block)
+    )(block, near, far)
 
 
 def attend_group(z, y, masked, query, kv, top, total, weighted):
@@ -400,18 +422,16 @@
     query,
     kv_src,
     out_src,
-    first_a,
-    cache_b,
+    near_first,
+    far_second,
     context,
     out_buf,
-    cache_dst_a,
-    cache_dst_b,
+    near_dst,
+    far_dst,
     kv_buf,
-    second_a,
-    first_b,
-    second_b,
-    relay_a,
-    relay_b,
+    near_second,
+    near_relay,
+    far_relay,
     top,
     total,
     weighted,
@@ -420,12 +440,10 @@
     greet(())
     kv = Flow(kv_src, kv_buf, HD, *sems[0:5])
     out = Gather(out_src, out_buf, 32, *sems[5:8])
-    half_a = Exchange(
-        ORDERS[0], (1, 2), (None, first_a, second_a, cache_dst_a), relay_a, *sems[8:11]
+    near = Exchange(
+        ORDERS[0], (1, 2), (None, near_first, near_second, near_dst), near_relay, *sems[8:11]
     )
-    half_b = Exchange(
-        ORDERS[1], (0, 1, 2), (cache_b, first_b, second_b, cache_dst_b), relay_b, *sems[11:14]
-    )
+    far = Exchange(FAR_ORDER, (2,), (None, None, far_second, far_dst), far_relay, *sems[11:14])
     my_z, my_y, _ = coordinates()
     state = (query, kv_buf, top, total, weighted)
 
@@ -444,7 +462,7 @@
     top[...] = jnp.full_like(top, LOWEST)
     total[...] = jnp.zeros_like(total)
     weighted[...] = jnp.zeros_like(weighted)
-    kv.head(lambda: half_b.start(0))
+    kv.head(lambda: far.start(2))
     out.own()
     attend_group(my_z, my_y, True, *state)
     kv.z_finish()
@@ -456,70 +474,61 @@
     kv.pass_on(2, 0)
     kv.finish(2, 0)
     kv.start(2, 1)
-    half_a.start(1)
+    near.start(1)
     out.pass_on(0)
     kv.finish(3, 1)
     row(3, 0)
     kv.pass_on(2, 1)
-    half_b.pass_on(0)
-    half_a.pass_on(1)
+    far.pass_on(2)
+    near.pass_on(1)
     out.finish(0)
     out.start(1)
     row(3, 1)
     kv.finish(1, 1)
     kv.finish(2, 1)
     out.pass_on(1)
-    half_a.finish(1)
-    half_a.start(2)
+    near.finish(1)
+    near.start(2)
     row(1, 0)
-    half_b.finish(0)
-    half_b.start(1)
-    half_a.pass_on(2)
+    near.pass_on(2)
     out.finish(1)
     out.start(2)
     row(1, 1)
-    half_b.pass_on(1)
     out.pass_on(2)
     row(2, 0)
-    half_b.finish(1)
-    half_b.start(2)
     row(2, 1)
-    half_b.pass_on(2)
     width = query.shape[1] // QPK
     for head in range(QPK):
         cols = pl.ds(head * width, width)
         context[pl.ds(head * HD, HD), :] = (weighted[:, cols] / total[:, cols]).astype(
             context.dtype
         )
-    half_a.finish(2)
-    half_b.finish(2)
+    near.finish(2)
+    far.finish(2)
     out.finish(2)
     kv.drain()
     out.drain()
-    half_a.drain()
-    half_b.drain()
-
-
-def attend(query, kv_block, out_block, first_a, cache_b):
+    near.drain()
+    far.drain()
+
+
+def attend(query, kv_block, out_block, near, far):
     columns = query.shape[1]
-    cache = pltpu.VMEM(cache_b.shape, cache_b.dtype)
     return pl.pallas_call(
         attend_kernel,
         out_shape=(
             jax.ShapeDtypeStruct((QPK * HD, columns // QPK), jnp.bfloat16),
             gathered(out_block),
-            like(first_a),
-            like(cache_b),
+            like(near),
+            like(far),
         ),
         in_specs=[VMEM_SPEC] * 5,
         out_specs=[VMEM_SPEC] * 4,
         scratch_shapes=[
             pltpu.VMEM(gathered(kv_block).shape, kv_block.dtype),
-            pltpu.VMEM(first_a.shape, first_a.dtype),
-            cache,
-            cache,
-            relay_buffer(first_a, 2),
-            relay_buffer(cache_b, 3),
+            pltpu.VMEM(near.shape, near.dtype),
+            relay_buffer(near, 2),
+            relay_buffer(far, 1),
             pltpu.VMEM((1, columns), jnp.float32),
             pltpu.VMEM((1, columns), jnp.float32),
             pltpu.VMEM((HD, columns), jnp.float32),
@@ -530,7 +539,7 @@
         ],
         compiler_params=pltpu.CompilerParams(collective_id=1, has_side_effects=True),
         name="attend",
-    )(query, kv_block, out_block, first_a, cache_b)
+    )(query, kv_block, out_block, near, far)
 
 
 def head_sum_kernel(part, result, swapped, pair, arrived, swap_sem, send_sem, recv_sem):
@@ -686,13 +695,13 @@
     hidden_in, norm_gain, w_qkv, w_out, prefill_cache, lengths, prefill_table, decode_table
 ):
     layers, slot_count, kv_local, extent = prefill_cache.shape
-    (cache_a, cache_b), origin = outgoing_blocks(
+    (near, far), origin = outgoing_blocks(
         prefill_cache, lengths, prefill_table, decode_table
     )
-    weights, first_a = gather_tok(pack_weight(w_qkv, 4, 80), cache_a, 48)
+    weights, near, far = gather_tok(pack_weight(w_qkv, 4, 80), near, far, 48)
     query, key_value = project(hidden_in, norm_gain, unpack_weight(weights, 4, *w_qkv.shape))
     context, out_all, *arrived = attend(
-        query, key_value, pack_weight(w_out.T, 3, 64), first_a, cache_b
+        query, key_value, pack_weight(w_out.T, 3, 64), near, far
     )
     out_weight = unpack_weight(out_all, 3, w_out.shape[1], w_out.shape[0])
     part = jnp.dot(out_weight, context, preferred_element_type=jnp.float32).astype(jnp.bfloat16)

time: 205 us -> 203 us (level)
  Pallas kernels: 180 us -> 175 us
  other arithmetic: 4.94 us -> 8.1 us
    pallas_call x1, Pallas kernels: 103 us -> 87.7 us  [attend(): pl.pallas_call(attend_kernel, out_shape=(jax.ShapeDtypeStruct((QPK * HD,...]
    pallas_call x1, Pallas kernels: 38.5 us -> 47 us  [gather_tok(): pl.pallas_call(functools.partial(gather_kernel, split), out_shape=(gather...]
    unnamed x28 -> x16, local copies, waits for them, and re-layouts: 4.18 us -> 5.86 us
where the time goes in v4:
time: 203 us; the launch traced here: 202 us
  Pallas kernels  175 us (86%)
  local copies, waits for them, and re-layouts  15.7 us (8%)
  other arithmetic  8.1 us (4%)
  matrix products  2.85 us (1%)
    pallas_call x1, Pallas kernels, attend(): pl.pallas_call(attend_kernel, out_shape=(jax.ShapeDtypeStruct((QPK * HD,...  87.7 us
    pallas_call x1, Pallas kernels, gather_tok(): pl.pallas_call(functools.partial(gather_kernel, split), out_shape=(gather...  47 us
    pallas_call x1, Pallas kernels, head_sum(): pl.pallas_call(head_sum_kernel, out_shape=jax.ShapeDtypeStruct(part.shape...  40.1 us
    unnamed x16, local copies, waits for them, and re-layouts  5.86 us

profile of v4, /device:TPU:449, one launch (start us, length us, event | category | flops | bytes accessed | tf_op | source)
XLA Modules:
  0.0 202.4 jit_solution(2169111574119027646)
XLA Ops:
  0.6 0.7 add_select_fusion
  1.4 1.1 fusion.11
  2.5 0.7 select_reduce_fusion.1
  3.4 0.3 broadcast_in_dim.91
  3.7 2.3 %fusion.7 = bf16[64,8,1280]{2,1,0:T(8,128)(2,1)S(1)} fusion(bf16[8,64,1,1280]{3,1,2,0:T(8,128)(2,1)} %param.14, pred[64,1280]{1,0:T(8,128)(4,1)S(1)} %broadcast_in_dim.91), kind=kLoop, calls=%fused_computation.17 | loop fusion | flops 655360 | bytes 2703360 | tf_op jit(solution)/shard_map/transpose | solution.py:688
  6.1 0.6 gather_fusion
  7.0 0.9 slice.47.far_src
  7.9 0.8 slice.46.near_src
  8.8 0.6 copy_bitcast_fusion.3
  9.4 47.0 %gather_tok.1 = (bf16[2,4,4,4,80,128]{5,4,3,2,1,0:T(8,128)(2,1)}, bf16[4,4,4,8,512]{4,3,2,1,0:T(8,128)(2,1)}, bf16[4,4,4,8,768]{4,3,2,1,0:T(8,128)(2,1)}) custom-call(bf16[2,80,128]{2,1,0:T(8,128)(2,1)} %bitcast.78, bf16[4,4,4,8,512]{4,3,2,1,0:T(8,128)(2,1)} %slice.46.near_src, bf16[4,4,4,8,768]{4,3,2,1,0:T(8,128)(2,1)} %slice.47.far_src), custom_call_target="tpu_custom_call" | custom-call | tf_op jit(solution)/shard_map/gather_tok/pallas_call | solution.py:365
  56.4 1.9 copy.38
  58.4 1.0 copy.39
  59.4 0.5 copy.57
  59.9 0.8 copy-done.1
  60.7 0.3 fusion
  61.1 0.9 fusion.3
  62.1 0.2 multiply_cosine_fusion
  62.4 0.6 maximum_bitcast_fusion.kv_src
  63.1 0.7 copy.49
  63.8 0.6 pad.14
  64.4 87.7 %attend.1 = (bf16[320,256]{1,0:T(8,128)(2,1)}, bf16[2,4,4,4,64,128]{5,4,3,2,1,0:T(8,128)(2,1)}, bf16[4,4,4,8,512]{4,3,2,1,0:T(8,128)(2,1)}, bf16[4,4,4,8,768]{4,3,2,1,0:T(8,128)(2,1)}) custom-call(bf16[80,1024]{1,0:T(8,128)(2,1)} %bitcast.74, bf16[2,160,128]{2,1,0:T(8,128)(2,1)} %maximum_bitcast_fusion.kv_src, bf16[2,64,128]{2,1,0:T(8,128)(2,1)} %bitcast.79, ...), custom_call_target="tpu_custom_call" | custom-call | tf_op jit(solution)/shard_map/attend/pallas_call | solution.py:517
  152.1 1.4 pad_maximum_fusion
  153.6 0.6 gather_fusion.1
  154.4 1.3 copy.46
  155.7 0.8 copy-done
  156.5 0.2 copy.44
  156.9 1.0 copy.45
  157.9 0.3 copy.58
  158.3 0.6 copy-done.4
  158.8 1.9 convolution_convert_fusion
  160.7 40.1 %head_sum.1 = bf16[320,256]{1,0:T(8,128)(2,1)} custom-call(bf16[4,2,320,256]{3,2,1,0:T(8,128)(2,1)} %bitcast.73), custom_call_target="tpu_custom_call" | custom-call | tf_op jit(solution)/shard_map/head_sum/pallas_call | solution.py:603
  200.8 1.6 copy.60
  (34 shorter events, 1.1 us)
Async XLA Ops:
  7.0 1.8 copy-start.2
  59.4 1.3 copy-start.1
  59.9 1.2 copy-start.5
  62.0 1.7 copy-start.3
  154.4 2.1 %copy-start = (bf16[2,4,4,4,64,128]{5,4,3,2,1,0:T(8,128)(2,1)S(1)}, bf16[2,4,4,4,64,128]{5,4,3,2,1,0:T(8,128)(2,1)}, u32[]{:S(2)}) copy-start(bf16[2,4,4,4,64,128]{5,4,3,2,1,0:T(8,128)(2,1)} %get-tuple-element.13) | copy-start | bytes 6291460
  157.9 0.9 copy-start.4

commit v5 on v4

--- a/solution.py
+++ b/solution.py
@@ -200,8 +200,6 @@
                         self.copy(row, part, phase, which).wait_send()
 
     def head(self, beside):
-        self.own()
-        self.z_start()
         self.start(0, 0)
         self.pass_on(0, 0)
         self.finish(0, 0)
@@ -300,6 +298,8 @@
         near.start(0)
         far.start(0)
 
+    gather.own()
+    gather.z_start()
     gather.head(beside)
     gather.z_finish()
     gather.start(2, 0)
@@ -462,39 +462,44 @@
     top[...] = jnp.full_like(top, LOWEST)
     total[...] = jnp.zeros_like(total)
     weighted[...] = jnp.zeros_like(weighted)
-    kv.head(lambda: far.start(2))
+    def beside():
+        out.pass_on(0)
+        far.start(2)
+
     out.own()
+    kv.own()
+    kv.z_start()
+    out.start(0)
+    kv.head(beside)
     attend_group(my_z, my_y, True, *state)
     kv.z_finish()
     kv.start(2, 0)
-    out.start(0)
     groups(my_z, 0, my_y)
     for way in (3, 1):
         kv.pass_on(way, 1)
     kv.pass_on(2, 0)
     kv.finish(2, 0)
     kv.start(2, 1)
+    out.finish(0)
+    out.start(1)
     near.start(1)
-    out.pass_on(0)
     kv.finish(3, 1)
     row(3, 0)
     kv.pass_on(2, 1)
-    far.pass_on(2)
-    near.pass_on(1)
-    out.finish(0)
-    out.start(1)
     row(3, 1)
     kv.finish(1, 1)
-    kv.finish(2, 1)
     out.pass_on(1)
+    near.pass_on(1)
+    row(1, 0)
+    far.pass_on(2)
     near.finish(1)
     near.start(2)
-    row(1, 0)
-    near.pass_on(2)
     out.finish(1)
     out.start(2)
     row(1, 1)
+    near.pass_on(2)
     out.pass_on(2)
+    kv.finish(2, 1)
     row(2, 0)
     row(2, 1)
     width = query.shape[1] // QPK

time: 203 us -> 205 us (level)
  Pallas kernels: 175 us -> 178 us
    pallas_call x1, Pallas kernels: 40.1 us -> 45.6 us  [head_sum(): pl.pallas_call(head_sum_kernel, out_shape=jax.ShapeDtypeStruct(part.shape...]
    pallas_call x1, Pallas kernels: 87.7 us -> 84.9 us  [attend(): pl.pallas_call(attend_kernel, out_shape=(jax.ShapeDtypeStruct((QPK * HD,...]
where the time goes in v5:
time: 205 us
  Pallas kernels  178 us (87%)
  local copies, waits for them, and re-layouts  15.7 us (8%)
  other arithmetic  8.1 us (4%)
  matrix products  2.85 us (1%)
    pallas_call x1, Pallas kernels, attend(): pl.pallas_call(attend_kernel, out_shape=(jax.ShapeDtypeStruct((QPK * HD,...  84.9 us
    pallas_call x1, Pallas kernels, gather_tok(): pl.pallas_call(functools.partial(gather_kernel, split), out_shape=(gather...  47 us
    pallas_call x1, Pallas kernels, head_sum(): pl.pallas_call(head_sum_kernel, out_shape=jax.ShapeDtypeStruct(part.shape...  45.6 us
    unnamed x16, local copies, waits for them, and re-layouts  5.86 us

profile of v5, /device:TPU:449, one launch (start us, length us, event | category | flops | bytes accessed | tf_op | source)
XLA Modules:
  0.0 205.1 jit_solution(4218794647652265158)
XLA Ops:
  0.6 0.7 add_select_fusion
  1.4 1.1 fusion.11
  2.5 0.7 select_reduce_fusion.1
  3.4 0.3 broadcast_in_dim.91
  3.7 2.3 %fusion.7 = bf16[64,8,1280]{2,1,0:T(8,128)(2,1)S(1)} fusion(bf16[8,64,1,1280]{3,1,2,0:T(8,128)(2,1)} %param.14, pred[64,1280]{1,0:T(8,128)(4,1)S(1)} %broadcast_in_dim.91), kind=kLoop, calls=%fused_computation.17 | loop fusion | flops 655360 | bytes 2703360 | tf_op jit(solution)/shard_map/transpose | solution.py:693
  6.1 0.6 gather_fusion
  7.0 0.9 slice.47.far_src
  7.9 0.8 slice.46.near_src
  8.8 0.6 copy_bitcast_fusion.3
  9.4 47.0 %gather_tok.1 = (bf16[2,4,4,4,80,128]{5,4,3,2,1,0:T(8,128)(2,1)}, bf16[4,4,4,8,512]{4,3,2,1,0:T(8,128)(2,1)}, bf16[4,4,4,8,768]{4,3,2,1,0:T(8,128)(2,1)}) custom-call(bf16[2,80,128]{2,1,0:T(8,128)(2,1)} %bitcast.78, bf16[4,4,4,8,512]{4,3,2,1,0:T(8,128)(2,1)} %slice.46.near_src, bf16[4,4,4,8,768]{4,3,2,1,0:T(8,128)(2,1)} %slice.47.far_src), custom_call_target="tpu_custom_call" | custom-call | tf_op jit(solution)/shard_map/gather_tok/pallas_call | solution.py:365
  56.4 1.9 copy.38
  58.4 1.0 copy.39
  59.4 0.5 copy.57
  59.9 0.8 copy-done.1
  60.7 0.3 fusion
  61.1 0.9 fusion.3
  62.1 0.2 multiply_cosine_fusion
  62.4 0.6 maximum_bitcast_fusion.kv_src
  63.1 0.7 copy.49
  63.8 0.6 pad.14
  64.4 84.9 %attend.1 = (bf16[320,256]{1,0:T(8,128)(2,1)}, bf16[2,4,4,4,64,128]{5,4,3,2,1,0:T(8,128)(2,1)}, bf16[4,4,4,8,512]{4,3,2,1,0:T(8,128)(2,1)}, bf16[4,4,4,8,768]{4,3,2,1,0:T(8,128)(2,1)}) custom-call(bf16[80,1024]{1,0:T(8,128)(2,1)} %bitcast.74, bf16[2,160,128]{2,1,0:T(8,128)(2,1)} %maximum_bitcast_fusion.kv_src, bf16[2,64,128]{2,1,0:T(8,128)(2,1)} %bitcast.79, ...), custom_call_target="tpu_custom_call" | custom-call | tf_op jit(solution)/shard_map/attend/pallas_call | solution.py:522
  149.4 1.4 pad_maximum_fusion
  150.8 0.6 gather_fusion.1
  151.6 1.3 copy.46
  152.9 0.8 copy-done
  153.7 0.2 copy.44
  154.1 1.0 copy.45
  155.1 0.3 copy.58
  155.5 0.6 copy-done.4
  156.1 1.9 convolution_convert_fusion
  158.0 45.6 %head_sum.1 = bf16[320,256]{1,0:T(8,128)(2,1)} custom-call(bf16[4,2,320,256]{3,2,1,0:T(8,128)(2,1)} %bitcast.73), custom_call_target="tpu_custom_call" | custom-call | tf_op jit(solution)/shard_map/head_sum/pallas_call | solution.py:608
  203.5 1.6 copy.60
  (34 shorter events, 1.1 us)
Async XLA Ops:
  7.0 1.8 copy-start.2
  59.4 1.3 copy-start.1
  59.9 1.2 copy-start.5
  62.0 1.7 copy-start.3
  151.6 2.1 %copy-start = (bf16[2,4,4,4,64,128]{5,4,3,2,1,0:T(8,128)(2,1)S(1)}, bf16[2,4,4,4,64,128]{5,4,3,2,1,0:T(8,128)(2,1)}, u32[]{:S(2)}) copy-start(bf16[2,4,4,4,64,128]{5,4,3,2,1,0:T(8,128)(2,1)} %get-tuple-element.13) | copy-start | bytes 6291460
  155.1 0.9 copy-start.4
